TPU v7x, 1024 devices: a whole 4x4x32 slice. The times are simulated.
1024 devices in a mesh: wide: 64 (over z_lo, y), narrow: 16 (over x, z_hi, core).
Axes of the slice: x: 4, y: 4, z: 32 (z_hi: 2, z_lo: 16; z = z_hi * 16 + z_lo), core: 2. Of those that a mesh axis runs over, the one named last changes fastest.
Arguments:
- chemical_fractions: float32 [53, 128, 128, 128], P(None, 'wide', 'narrow'), may hold values from 0.1 to 1
- thermal_state: float32 [128, 128, 128], P('wide', 'narrow'), may hold values from 1 to 3
- ignited_stacks: int32 [128, 128], P('wide', 'narrow'), may hold values from 0 to 1, as said below
- spreading_number: float32 [53], replicated, may hold values from 0.02 to 0.15
- natural_exponent_scale: float32 [325], replicated, may hold values from -1 to 1
- arrhenius_energy: float32 [325], replicated, may hold values from 0.5 to 2
- incoming_stoichiometry: int32 [325, 53], replicated, may hold values 0 or 1
- outgoing_stoichiometry: int32 [325, 53], replicated, may hold values 0 or 1
Outputs:
- updated: float32 [53, 128, 128, 128], P(None, 'wide', 'narrow')
Inputs may be any that keep to these rules, and one draw needn't show every extreme that they name: `ignited_stacks`: on each device either 8 or 2 of its columns burn. In every group of devices along narrow, those with 8 burning columns are a quarter of the group and consecutive in index, with wrap-around.
All inputs are finite; a program needn't handle non-finite values.
Results may differ from a plain program's by a relative error of at most 0.0001.
Values sent between devices are 32-bit elements; how exact they have to be, the bound alone decides.
No kernel may reach another device: no remote copies, remote signals or barrier semaphores. Data moves between devices by JAX's collectives and lax.ppermute only.
A program may use at most 32 MiB of HBM per device.

v0:
```python
import jax
import jax.numpy as jnp
from jax import lax
from jax.experimental import pallas as pl
from jax.experimental.pallas import tpu as pltpu
from jax.sharding import PartitionSpec as P


BURN_MAX = 8
S = 53
R = 325
SP = 64
RP = 328
H = 128


VM = pl.BlockSpec(memory_space=pltpu.VMEM)
SM = pl.BlockSpec(memory_space=pltpu.SMEM)


def pack_kernel(x, long_out, short_out, up_out, down_out):
    p = lax.axis_index("narrow") % 2
    long_near = jnp.where(p == 0, 0, 7)
    long_far = jnp.where(p == 0, 1, 6)
    short_near = 7 - long_near
    short_far = 7 - long_far
    for r, row_out in ((0, down_out), (1, up_out)):
        long_edge = x[:, r, pl.ds(long_near, 1), :]
        short_edge = x[:, r, pl.ds(short_near, 1), :]
        long_out[:, r : r + 1, :] = long_edge
        short_out[:, r : r + 1, :] = short_edge
        row_out[:, 0:1, :] = long_edge
        row_out[:, 1:2, :] = short_edge
        long_out[:, 2 + r : 3 + r, :] = x[:, r, pl.ds(long_far, 1), :]
        short_out[:, 2 + r : 3 + r, :] = x[:, r, pl.ds(short_far, 1), :]


def fold_kernel(long, short, below, above, long_out, short_out):
    long_out[:, 0:2, :] = long[:, 0:2, :]
    short_out[:, 0:2, :] = short[:, 0:2, :]
    w = lax.axis_index("wide")
    low = jnp.where(w == 0, 0.0, 2.0)
    high = jnp.where(w == lax.axis_size("wide") - 1, 0.0, 2.0)
    long_out[:, 2:3, :] = long[:, 2:3, :] + low * below[:, 0:1, :]
    long_out[:, 3:4, :] = long[:, 3:4, :] + high * above[:, 0:1, :]
    short_out[:, 2:3, :] = short[:, 2:3, :] + low * below[:, 1:2, :]
    short_out[:, 3:4, :] = short[:, 3:4, :] + high * above[:, 1:2, :]


def first_edge_kernel(up, out):
    at = jnp.where(lax.axis_index("narrow") % 2 == 0, 7, 0)
    out[...] = up[:, 1, pl.ds(at, 1), :]


def edge_kernel(up, down, out):
    at = jnp.where(lax.axis_index("narrow") % 2 == 0, 7, 0)
    first = lax.axis_index("wide") == 0
    out[...] = jnp.where(first, up[:, 1, pl.ds(at, 1), :], down[:, 0, pl.ds(at, 1), :])


def around(v):
    return pltpu.roll(v, 1, 1) + pltpu.roll(v, H - 1, 1)


def final_kernel(
    marks,
    spread,
    x,
    up_0,
    up_1,
    down_0,
    down_1,
    short,
    long_d,
    long_b,
    long_c,
    diag_below,
    diag_above,
    across_a,
    across_b,
    corner_0,
    corner_1,
    temps,
    rate,
    left,
    right,
    out,
    index,
    stack,
):
    w = lax.axis_index("wide")
    p = lax.axis_index("narrow") % 2
    last = lax.axis_size("wide") - 1
    even = p == 0
    at_first = w == 0
    at_last = w == last
    sub = lax.broadcasted_iota(jnp.int32, (8, H), 0)
    is_lo = sub == 0
    is_hi = sub == 7
    long_edge = jnp.where(even, 0, 7)
    long_first = sub == jnp.where(at_first, long_edge, 8)
    long_last = sub == jnp.where(at_last, long_edge, 8)
    short_first = sub == jnp.where(at_first, 7 - long_edge, 8)
    short_last = sub == jnp.where(at_last, 7 - long_edge, 8)

    def beside(v, lo, hi):
        down = jnp.where(is_lo, lo, pltpu.roll(v, 1, 0))
        up = jnp.where(is_hi, hi, pltpu.roll(v, 7, 0))
        return down + up

    for s in range(S):
        c = spread[s]
        v0 = x[s, 0]
        v1 = x[s, 1]
        below_rows = up_0[s] + up_1[s]
        above_rows = down_0[s] + down_1[s]
        below_far = below_rows[0]
        below = below_rows[1]
        above = above_rows[0]
        above_far = above_rows[1]
        near_corner = 2.0 * (corner_0[s] + corner_1[s])
        below_far = below_far + jnp.where(long_first, 2.0 * (diag_below[s, 0:1, :] + across_a[s, 0:1, :]), 0.0)
        above_far = above_far + jnp.where(long_last, 2.0 * (diag_above[s, 0:1, :] + across_b[s, 0:1, :]), 0.0)
        below_far = below_far + jnp.where(short_first, near_corner, 0.0)
        above_far = above_far + jnp.where(short_last, near_corner, 0.0)
        long_s = long_d[s] + long_b[s] + long_c[s]
        lo = jnp.where(even, long_s, short[s])
        hi = jnp.where(even, short[s], long_s)
        u_lo = []
        u_hi = []
        for r in range(2):
            v = (v0, v1)[r]
            for side, edge, got in ((lo, 0, u_lo), (hi, 7, u_hi)):
                near = side[r : r + 1]
                n = side[2 + r : 3 + r] + side[1 - r : 2 - r] + v[edge : edge + 1] + around(near)
                got.append(near + c * (n - 6.0 * near))
        u0 = v0 + c * (below + v1 + beside(v0, lo[0:1], hi[0:1]) + around(v0) - 6.0 * v0)
        u1 = v1 + c * (v0 + above + beside(v1, lo[1:2], hi[1:2]) + around(v1) - 6.0 * v1)
        ub = below + c * (below_far + v0 + beside(below, 0.0, 0.0) + around(below) - 6.0 * below)
        ua = above + c * (above_far + v1 + beside(above, 0.0, 0.0) + around(above) - 6.0 * above)
        m0 = u0 + c * (ub + u1 + beside(u0, u_lo[0], u_hi[0]) + around(u0) - 6.0 * u0)
        m1 = u1 + c * (u0 + ua + beside(u1, u_lo[1], u_hi[1]) + around(u1) - 6.0 * u1)
        out[16 * s : 16 * s + 8, :] = m0
        out[16 * s + 8 : 16 * s + 16, :] = m1

    count = 0
    for col in range(16):
        index[count] = col
        count = count + marks[col // 8, col % 8]

    stack[...] = jnp.zeros(stack.shape, jnp.bfloat16)

    def react(cols):
        n = cols * H
        where = [index[i] for i in range(cols)]
        v = jnp.concatenate([out[pl.ds(i, S, stride=16), :] for i in where], axis=1)
        inv = 1.0 / jnp.concatenate([temps[pl.ds(i, 1), :] for i in where], axis=1)
        base = rate[:, 0:1] - rate[:, 1:2] * inv
        for _ in range(2):
            logs = jnp.log(v)
            top = logs.astype(jnp.bfloat16)
            rest = logs - top.astype(jnp.float32)
            mid = rest.astype(jnp.bfloat16)
            low = (rest - mid.astype(jnp.float32)).astype(jnp.bfloat16)
            stack[0:S, :n] = top
            stack[SP : SP + S, :n] = mid
            stack[2 * SP : 2 * SP + S, :n] = low
            expo = base + jnp.dot(left[...], stack[:, :n], preferred_element_type=jnp.float32)
            rates = jnp.exp(expo)
            top = rates.astype(jnp.bfloat16)
            low = (rates - top.astype(jnp.float32)).astype(jnp.bfloat16)
            both = jnp.dot(right[...], top, preferred_element_type=jnp.float32)
            both = both + jnp.dot(right[...], low, preferred_element_type=jnp.float32)
            v = v * (v + 0.5 * both[0:S]) / (v + 0.5 * both[SP : SP + S])
        for k, i in enumerate(where):
            out[pl.ds(i, S, stride=16), :] = v[:, k * H : (k + 1) * H]

    few = BURN_MAX // 4

    @pl.when(count > few)
    def _():
        react(BURN_MAX)

    @pl.when(count <= few)
    def _():
        react(few)


def sds(*shape):
    return jax.ShapeDtypeStruct(shape, jnp.float32)


def vds(*shape):
    return pltpu.VMEM(shape, jnp.float32)


def vmem(value):
    return pltpu.with_memory_space_constraint(value, pltpu.VMEM)


def shards(
    chemical_fractions,
    thermal_state,
    ignited_stacks,
    spreading_number,
    natural_exponent_scale,
    arrhenius_energy,
    incoming_stoichiometry,
    outgoing_stoichiometry,
):
    x = chemical_fractions
    nw = lax.axis_size("wide")
    nn = lax.axis_size("narrow")
    up = [(i, i + 1) for i in range(nw - 1)]
    down = [(i + 1, i) for i in range(nw - 1)]
    partner = [(i + 1) % nn if i % 2 else (i - 1) % nn for i in range(nn)]
    both = ("wide", "narrow")
    end = nw - 1
    half = nw // 2
    early = [i for i in range(nn) if i // 2 % 2 == 0]
    late = [i for i in range(nn) if i // 2 % 2 == 1]

    def at(i, j):
        return i * nn + j

    bf = jnp.bfloat16
    pad = ((0, RP - R), (0, SP - S))
    react_mat = jnp.pad(incoming_stoichiometry.astype(bf), pad)
    prod_mat = jnp.pad(outgoing_stoichiometry.astype(bf), pad)
    left = jnp.concatenate([react_mat] * 3, axis=1)
    right = jnp.concatenate([prod_mat, react_mat], axis=1).T
    rate = jnp.stack([natural_exponent_scale, arrhenius_energy], axis=1)
    rate = jnp.pad(rate, ((0, RP - R), (0, 0)))

    first_half = [(i, j) for i in range(half - 1) for j in early]
    others = [(i, j) for i in range(end) for j in range(nn) if i >= half - 1 or j in late]
    up_0 = lax.ppermute(
        x,
        both,
        [(at(i, j), at(i + 1, j)) for i, j in first_half]
        + [(at(end, j), at(0, j)) for j in early],
    )
    down_0 = lax.ppermute(x, both, [(at(i + 1, j), at(i, j)) for i, j in first_half])
    long_raw, short_raw, up_msg, down_msg = pl.pallas_call(
        pack_kernel,
        out_shape=(vds(S, 4, H), vds(S, 4, H), vds(S, 2, H), vds(S, 2, H)),
        in_specs=[VM],
        out_specs=(VM,) * 4,
        name="pack",
    )(x)
    corner_below = lax.ppermute(
        up_msg,
        both,
        [(at(a, j), at(b, j)) for a, b in up for j in range(nn)]
        + [(at(end, partner[j]), at(0, j)) for j in late],
    )
    corner_above = lax.ppermute(
        down_msg,
        both,
        [(at(a, j), at(b, j)) for a, b in down for j in range(nn)]
        + [(at(0, j), at(end, partner[j])) for j in late],
    )
    across_a = lax.ppermute(up_msg, both, [(at(end, partner[j]), at(0, j)) for j in early])
    across_b = lax.ppermute(down_msg, both, [(at(0, j), at(end, partner[j])) for j in early])
    long_msg, short_msg = pl.pallas_call(
        fold_kernel,
        out_shape=(vds(S, 4, H), vds(S, 4, H)),
        in_specs=[VM] * 4,
        out_specs=(VM,) * 2,
        name="fold",
    )(vmem(long_raw), vmem(short_raw), vmem(corner_below), vmem(corner_above))

    def long_swap(senders):
        return lax.ppermute(long_msg, both, [(at(i, j), at(i, partner[j])) for i, j in senders])

    long_b = long_swap([(i, j) for i in range(end) for j in range(nn) if i or j in late])
    up_1 = lax.ppermute(
        x,
        both,
        [(at(i, j), at(i + 1, j)) for i, j in others] + [(at(end, j), at(0, j)) for j in late],
    )
    down_1 = lax.ppermute(
        x,
        both,
        [(at(i + 1, j), at(i, j)) for i, j in others]
        + [(at(0, j), at(end, j)) for j in range(nn)],
    )
    short_msg, left, right, rate = lax.optimization_barrier((short_msg, left, right, rate))
    short = lax.ppermute(short_msg, "narrow", [(j, j ^ 1) for j in range(nn)])
    long_c = long_swap([(0, j) for j in early])
    long_d = long_swap([(end, j) for j in range(nn)])
    edge_0 = pl.pallas_call(
        first_edge_kernel,
        out_shape=vds(S, 1, H),
        in_specs=[VM],
        out_specs=VM,
        name="edge_0",
    )(vmem(up_0))
    corner_0 = lax.ppermute(edge_0, both, [(at(0, j), at(0, j ^ 1)) for j in early])
    edge_1 = pl.pallas_call(
        edge_kernel,
        out_shape=vds(S, 1, H),
        in_specs=[VM] * 2,
        out_specs=VM,
        name="edge_1",
    )(vmem(up_1), vmem(down_1))
    corner_1 = lax.ppermute(
        edge_1,
        both,
        [(at(0, j), at(0, j ^ 1)) for j in late] + [(at(end, j), at(end, j ^ 1)) for j in range(nn)],
    )

    out = pl.pallas_call(
        final_kernel,
        out_shape=sds(S * 16, H),
        in_specs=[SM, SM] + [VM] * 19,
        out_specs=VM,
        scratch_shapes=[pltpu.SMEM((17,), jnp.int32), pltpu.VMEM((3 * SP, BURN_MAX * H), bf)],
        name="step",
    )(
        ignited_stacks,
        spreading_number,
        x,
        vmem(up_0),
        vmem(up_1),
        vmem(down_0),
        vmem(down_1),
        vmem(short),
        vmem(long_d),
        vmem(long_b),
        vmem(long_c),
        vmem(corner_below),
        vmem(corner_above),
        vmem(across_a),
        vmem(across_b),
        vmem(corner_0),
        vmem(corner_1),
        thermal_state.reshape(16, H),
        rate,
        left,
        right,
    )
    return out.reshape(S, 2, 8, H)


def solution(mesh):
    in_specs = (
        P(None, "wide", "narrow", None),
        P("wide", "narrow", None),
        P("wide", "narrow"),
        P(),
        P(),
        P(),
        P(),
        P(),
    )
    out_specs = P(None, "wide", "narrow", None)
    return jax.shard_map(shards, mesh=mesh, in_specs=in_specs, out_specs=out_specs, check_vma=False)
```

profile of v0, /device:TPU:6, one launch (start us, length us, event | category | flops | bytes accessed | tf_op | source)
XLA Modules:
  0.0 122.7 jit_solution(14681026574875778135)
XLA Ops:
  0.0 0.0 copy-start
  0.0 29.0 %collective-permute-start.3 = (f32[53,2,8,128]{3,2,1,0:T(8,128)}, f32[53,2,8,128]{3,2,1,0:T(8,128)S(1)}, u32[]{:S(2)}, u32[]{:S(2)}) collective-permute-start(f32[53,2,8,128]{3,2,1,0:T(8,128)} %x.9), channel_id=1, source_target_pairs={{18,2},{19,3},{22,6},{23,7},{26,10},{27,11},{30,14},{31,15},{34,18... | collective-permute-start | bytes 1302536 | tf_op jit(solution)/shard_map/ppermute | solution.py:282
  29.0 0.7 collective-permute-start.1
  29.7 1.9 %collective-permute-start = (f32[53,2,8,128]{3,2,1,0:T(8,128)}, f32[53,2,8,128]{3,2,1,0:T(8,128)S(1)}, u32[]{:S(2)}, u32[]{:S(2)}) collective-permute-start(f32[53,2,8,128]{3,2,1,0:T(8,128)} %x.9), channel_id=1, source_target_pairs={{0,16},{1,17},{4,20},{5,21},{8,24},{9,25},{12,28},{13,29},{16,32},... | collective-permute-start | bytes 1302536 | tf_op jit(solution)/shard_map/ppermute | solution.py:237
  31.6 1.2 pack.1
  32.9 1.3 %collective-permute-start.10 = (f32[53,2,128]{2,1,0:T(2,128)S(1)}, f32[53,2,128]{2,1,0:T(2,128)S(1)}, u32[]{:S(2)}, u32[]{:S(2)}) collective-permute-start(f32[53,2,128]{2,1,0:T(2,128)S(1)} %get-tuple-element.17), channel_id=1, source_target_pairs={{1023,0},{1010,1},{1011,4},{1014,5},{1015,8},{1018,9},{1019,12},{1... | collective-permute-start | bytes 162824 | tf_op jit(solution)/shard_map/ppermute | solution.py:263
  34.2 1.3 %collective-permute-start.4 = (f32[53,2,128]{2,1,0:T(2,128)S(1)}, f32[53,2,128]{2,1,0:T(2,128)S(1)}, u32[]{:S(2)}, u32[]{:S(2)}) collective-permute-start(f32[53,2,128]{2,1,0:T(2,128)S(1)} %get-tuple-element.17), channel_id=1, source_target_pairs={{0,16},{1,17},{2,18},{3,19},{4,20},{5,21},{6,22},{7,23},{8,24},{9,... | collective-permute-start | bytes 162824 | tf_op jit(solution)/shard_map/ppermute | solution.py:251
  35.5 0.0 copy-done
  35.5 0.0 copy-start.1
  35.5 12.2 %collective-permute-done.10.across_a = f32[53,2,128]{2,1,0:T(2,128)S(1)} collective-permute-done((f32[53,2,128]{2,1,0:T(2,128)S(1)}, f32[53,2,128]{2,1,0:T(2,128)S(1)}, u32[]{:S(2)}, u32[]{:S(2)}) %collective-permute-start.10) | collective-permute-done | bytes 54304 | tf_op jit(solution)/shard_map/ppermute | solution.py:263
  47.7 1.3 %collective-permute-start.2 = (f32[53,2,8,128]{3,2,1,0:T(8,128)}, f32[53,2,8,128]{3,2,1,0:T(8,128)S(1)}, u32[]{:S(2)}, u32[]{:S(2)}) collective-permute-start(f32[53,2,8,128]{3,2,1,0:T(8,128)} %x.9), channel_id=1, source_target_pairs={{16,0},{17,1},{20,4},{21,5},{24,8},{25,9},{28,12},{29,13},{32,16},... | collective-permute-start | bytes 1302536 | tf_op jit(solution)/shard_map/ppermute | solution.py:243
  49.0 0.0 copy-done.1
  49.0 0.0 collective-permute-done.4.below.diag_below
  49.0 0.0 copy-start.2
  49.0 1.3 %collective-permute-start.5 = (f32[53,2,128]{2,1,0:T(2,128)S(1)}, f32[53,2,128]{2,1,0:T(2,128)S(1)}, u32[]{:S(2)}, u32[]{:S(2)}) collective-permute-start(f32[53,2,128]{2,1,0:T(2,128)S(1)} %get-tuple-element.18), channel_id=1, source_target_pairs={{16,0},{17,1},{18,2},{19,3},{20,4},{21,5},{22,6},{23,7},{24,8},{25... | collective-permute-start | bytes 162824 | tf_op jit(solution)/shard_map/ppermute | solution.py:257
  50.3 0.6 fusion.2.right
  51.0 0.0 copy-done.2
  51.0 0.0 copy-start.3
  51.0 0.7 copy-done.3
  51.7 12.1 %collective-permute-done.5.above.diag_above = f32[53,2,128]{2,1,0:T(2,128)S(1)} collective-permute-done((f32[53,2,128]{2,1,0:T(2,128)S(1)}, f32[53,2,128]{2,1,0:T(2,128)S(1)}, u32[]{:S(2)}, u32[]{:S(2)}) %collective-permute-start.5) | collective-permute-done | bytes 54304 | tf_op jit(solution)/shard_map/ppermute | solution.py:257
  63.8 1.3 %collective-permute-start.11 = (f32[53,2,128]{2,1,0:T(2,128)S(1)}, f32[53,2,128]{2,1,0:T(2,128)S(1)}, u32[]{:S(2)}, u32[]{:S(2)}) collective-permute-start(f32[53,2,128]{2,1,0:T(2,128)S(1)} %get-tuple-element.18), channel_id=1, source_target_pairs={{0,1023},{1,1010},{4,1011},{5,1014},{8,1015},{9,1018},{12,1019},{1... | collective-permute-start | bytes 162824 | tf_op jit(solution)/shard_map/ppermute | solution.py:264
  65.1 0.1 copy.13
  65.3 0.7 pad.13.rate
  65.9 0.2 fold.1
  66.1 16.4 %collective-permute-done.11.across_b = f32[53,2,128]{2,1,0:T(2,128)S(1)} collective-permute-done((f32[53,2,128]{2,1,0:T(2,128)S(1)}, f32[53,2,128]{2,1,0:T(2,128)S(1)}, u32[]{:S(2)}, u32[]{:S(2)}) %collective-permute-start.11) | collective-permute-done | bytes 54304 | tf_op jit(solution)/shard_map/ppermute | solution.py:264
  82.5 1.9 %collective-permute-start.6 = (f32[53,4,128]{2,1,0:T(4,128)S(1)}, f32[53,4,128]{2,1,0:T(4,128)S(1)}, u32[]{:S(2)}, u32[]{:S(2)}) collective-permute-start(f32[53,4,128]{2,1,0:T(4,128)S(1)} %get-tuple-element.20), channel_id=1, source_target_pairs={{0,1},{1,0},{2,3},{3,2},{4,5},{5,4},{6,7},{7,6},{8,9},{9,8},{10,11... | collective-permute-start | bytes 325640 | tf_op jit(solution)/shard_map/ppermute | solution.py:289
  84.4 0.0 collective-permute-done.3.down.down_1
  84.5 4.1 %collective-permute-start.9 = (f32[53,4,128]{2,1,0:T(4,128)S(1)}, f32[53,4,128]{2,1,0:T(4,128)S(1)}, u32[]{:S(2)}, u32[]{:S(2)}) collective-permute-start(f32[53,4,128]{2,1,0:T(4,128)S(1)} %get-tuple-element.21), channel_id=1, source_target_pairs={{0,15},{1,2},{4,3},{5,6},{8,7},{9,10},{12,11},{13,14}} | collective-permute-start | bytes 325640 | tf_op jit(solution)/shard_map/ppermute | solution.py:274
  88.6 0.0 collective-permute-done.1.up.up_1
  88.6 1.3 %collective-permute-start.8 = (f32[53,4,128]{2,1,0:T(4,128)S(1)}, f32[53,4,128]{2,1,0:T(4,128)S(1)}, u32[]{:S(2)}, u32[]{:S(2)}) collective-permute-start(f32[53,4,128]{2,1,0:T(4,128)S(1)} %get-tuple-element.21), channel_id=1, source_target_pairs={{2,1},{3,4},{6,5},{7,8},{10,9},{11,12},{14,13},{15,0},{16,31},{17,... | collective-permute-start | bytes 325640 | tf_op jit(solution)/shard_map/ppermute | solution.py:274
  89.9 0.0 collective-permute-done.up.up_0
  89.9 0.7 collective-permute-start.7
  90.6 0.0 collective-permute-done.6.short
  90.7 0.7 collective-permute-start.13
  91.3 0.0 collective-permute-done.9.long_c
  91.4 2.0 %collective-permute-start.12 = (f32[53,1,128]{2,1,0:T(1,128)S(1)}, f32[53,1,128]{2,1,0:T(1,128)S(1)}, u32[]{:S(2)}, u32[]{:S(2)}) collective-permute-start(f32[53,1,128]{2,1,0:T(1,128)S(1)} %edge_0.1), channel_id=1, source_target_pairs={{0,1},{1,0},{4,5},{5,4},{8,9},{9,8},{12,13},{13,12}} | collective-permute-start | bytes 81416 | tf_op jit(solution)/shard_map/ppermute | solution.py:299
  93.4 0.8 copy.14.left
  94.2 20.5 %collective-permute-done.8.long_b = f32[53,4,128]{2,1,0:T(4,128)S(1)} collective-permute-done((f32[53,4,128]{2,1,0:T(4,128)S(1)}, f32[53,4,128]{2,1,0:T(4,128)S(1)}, u32[]{:S(2)}, u32[]{:S(2)}) %collective-permute-start.8) | collective-permute-done | bytes 108576 | tf_op jit(solution)/shard_map/ppermute | solution.py:274
  114.7 0.0 collective-permute-done.7.long_d
  114.7 0.0 collective-permute-done.2.down_0
  114.7 0.0 collective-permute-done.13.corner_1
  114.7 0.0 collective-permute-done.12.corner_0
  114.7 8.0 %step.1 = f32[848,128]{1,0:T(8,128)} custom-call(s32[2,8]{1,0:T(2,128)} %marks.1, f32[53]{0:T(128)} %spread.1, f32[53,2,8,128]{3,2,1,0:T(8,128)} %x.9, f32[53,2,8,128]{3,2,1,0:T(8,128)S(1)} %collective-permute-done.up.up_0, f32[53,2,8,128]{3,2,1,0:T(8,128)S(1)} %collective-permute-done.1.up.up_1, f32[53,2,8,128]{3,2,1,0:T(8,128)S(1)} %collective-permute-done.2.down_0, ...), custom_call_target="tpu_custom_call" | custom-call | tf_op jit(solution)/shard_map/step/pallas_call | solution.py:313
  (9 shorter events, 0.1 us)
Async XLA Ops:
  0.0 35.5 %copy-start = (s32[325,53]{0,1:T(8,128)S(1)}, s32[325,53]{0,1:T(8,128)}, u32[]{:S(2)}) copy-start(s32[325,53]{0,1:T(8,128)} %param.14) | copy-start | bytes 206704
  0.0 84.4 %collective-permute-start.3 = (f32[53,2,8,128]{3,2,1,0:T(8,128)}, f32[53,2,8,128]{3,2,1,0:T(8,128)S(1)}, u32[]{:S(2)}, u32[]{:S(2)}) collective-permute-start(f32[53,2,8,128]{3,2,1,0:T(8,128)} %x.9), channel_id=1, source_target_pairs={{18,2},{19,3},{22,6},{23,7},{26,10},{27,11},{30,14},{31,15},{34,18... | collective-permute-start | bytes 1302536 | tf_op jit(solution)/shard_map/ppermute | solution.py:282
  29.0 59.5 %collective-permute-start.1 = (f32[53,2,8,128]{3,2,1,0:T(8,128)}, f32[53,2,8,128]{3,2,1,0:T(8,128)S(1)}, u32[]{:S(2)}, u32[]{:S(2)}) collective-permute-start(f32[53,2,8,128]{3,2,1,0:T(8,128)} %x.9), channel_id=1, source_target_pairs={{2,18},{3,19},{6,22},{7,23},{10,26},{11,27},{14,30},{15,31},{18,34... | collective-permute-start | bytes 1302536 | tf_op jit(solution)/shard_map/ppermute | solution.py:277
  29.7 60.2 %collective-permute-start = (f32[53,2,8,128]{3,2,1,0:T(8,128)}, f32[53,2,8,128]{3,2,1,0:T(8,128)S(1)}, u32[]{:S(2)}, u32[]{:S(2)}) collective-permute-start(f32[53,2,8,128]{3,2,1,0:T(8,128)} %x.9), channel_id=1, source_target_pairs={{0,16},{1,17},{4,20},{5,21},{8,24},{9,25},{12,28},{13,29},{16,32},... | collective-permute-start | bytes 1302536 | tf_op jit(solution)/shard_map/ppermute | solution.py:237
  32.9 14.8 %collective-permute-start.10 = (f32[53,2,128]{2,1,0:T(2,128)S(1)}, f32[53,2,128]{2,1,0:T(2,128)S(1)}, u32[]{:S(2)}, u32[]{:S(2)}) collective-permute-start(f32[53,2,128]{2,1,0:T(2,128)S(1)} %get-tuple-element.17), channel_id=1, source_target_pairs={{1023,0},{1010,1},{1011,4},{1014,5},{1015,8},{1018,9},{1019,12},{1... | collective-permute-start | bytes 162824 | tf_op jit(solution)/shard_map/ppermute | solution.py:263
  34.2 14.9 %collective-permute-start.4 = (f32[53,2,128]{2,1,0:T(2,128)S(1)}, f32[53,2,128]{2,1,0:T(2,128)S(1)}, u32[]{:S(2)}, u32[]{:S(2)}) collective-permute-start(f32[53,2,128]{2,1,0:T(2,128)S(1)} %get-tuple-element.17), channel_id=1, source_target_pairs={{0,16},{1,17},{2,18},{3,19},{4,20},{5,21},{6,22},{7,23},{8,24},{9,... | collective-permute-start | bytes 162824 | tf_op jit(solution)/shard_map/ppermute | solution.py:251
  35.5 13.5 %copy-start.1 = (s32[325,53]{0,1:T(8,128)S(1)}, s32[325,53]{0,1:T(8,128)}, u32[]{:S(2)}) copy-start(s32[325,53]{0,1:T(8,128)} %param.15) | copy-start | bytes 206704
  47.7 67.0 %collective-permute-start.2 = (f32[53,2,8,128]{3,2,1,0:T(8,128)}, f32[53,2,8,128]{3,2,1,0:T(8,128)S(1)}, u32[]{:S(2)}, u32[]{:S(2)}) collective-permute-start(f32[53,2,8,128]{3,2,1,0:T(8,128)} %x.9), channel_id=1, source_target_pairs={{16,0},{17,1},{20,4},{21,5},{24,8},{25,9},{28,12},{29,13},{32,16},... | collective-permute-start | bytes 1302536 | tf_op jit(solution)/shard_map/ppermute | solution.py:243
  49.0 2.0 %copy-start.2 = (f32[325]{0:T(512)S(1)}, f32[325]{0:T(512)}, u32[]{:S(2)}) copy-start(f32[325]{0:T(512)} %param.12) | copy-start | bytes 3904
  49.0 14.8 %collective-permute-start.5 = (f32[53,2,128]{2,1,0:T(2,128)S(1)}, f32[53,2,128]{2,1,0:T(2,128)S(1)}, u32[]{:S(2)}, u32[]{:S(2)}) collective-permute-start(f32[53,2,128]{2,1,0:T(2,128)S(1)} %get-tuple-element.18), channel_id=1, source_target_pairs={{16,0},{17,1},{18,2},{19,3},{20,4},{21,5},{22,6},{23,7},{24,8},{25... | collective-permute-start | bytes 162824 | tf_op jit(solution)/shard_map/ppermute | solution.py:257
  51.0 0.7 copy-start.3
  63.8 18.7 %collective-permute-start.11 = (f32[53,2,128]{2,1,0:T(2,128)S(1)}, f32[53,2,128]{2,1,0:T(2,128)S(1)}, u32[]{:S(2)}, u32[]{:S(2)}) collective-permute-start(f32[53,2,128]{2,1,0:T(2,128)S(1)} %get-tuple-element.18), channel_id=1, source_target_pairs={{0,1023},{1,1010},{4,1011},{5,1014},{8,1015},{9,1018},{12,1019},{1... | collective-permute-start | bytes 162824 | tf_op jit(solution)/shard_map/ppermute | solution.py:264
  82.5 8.1 %collective-permute-start.6 = (f32[53,4,128]{2,1,0:T(4,128)S(1)}, f32[53,4,128]{2,1,0:T(4,128)S(1)}, u32[]{:S(2)}, u32[]{:S(2)}) collective-permute-start(f32[53,4,128]{2,1,0:T(4,128)S(1)} %get-tuple-element.20), channel_id=1, source_target_pairs={{0,1},{1,0},{2,3},{3,2},{4,5},{5,4},{6,7},{7,6},{8,9},{9,8},{10,11... | collective-permute-start | bytes 325640 | tf_op jit(solution)/shard_map/ppermute | solution.py:289
  84.5 6.9 %collective-permute-start.9 = (f32[53,4,128]{2,1,0:T(4,128)S(1)}, f32[53,4,128]{2,1,0:T(4,128)S(1)}, u32[]{:S(2)}, u32[]{:S(2)}) collective-permute-start(f32[53,4,128]{2,1,0:T(4,128)S(1)} %get-tuple-element.21), channel_id=1, source_target_pairs={{0,15},{1,2},{4,3},{5,6},{8,7},{9,10},{12,11},{13,14}} | collective-permute-start | bytes 325640 | tf_op jit(solution)/shard_map/ppermute | solution.py:274
  88.6 26.1 %collective-permute-start.8 = (f32[53,4,128]{2,1,0:T(4,128)S(1)}, f32[53,4,128]{2,1,0:T(4,128)S(1)}, u32[]{:S(2)}, u32[]{:S(2)}) collective-permute-start(f32[53,4,128]{2,1,0:T(4,128)S(1)} %get-tuple-element.21), channel_id=1, source_target_pairs={{2,1},{3,4},{6,5},{7,8},{10,9},{11,12},{14,13},{15,0},{16,31},{17,... | collective-permute-start | bytes 325640 | tf_op jit(solution)/shard_map/ppermute | solution.py:274
  89.9 24.8 %collective-permute-start.7 = (f32[53,4,128]{2,1,0:T(4,128)S(1)}, f32[53,4,128]{2,1,0:T(4,128)S(1)}, u32[]{:S(2)}, u32[]{:S(2)}) collective-permute-start(f32[53,4,128]{2,1,0:T(4,128)S(1)} %get-tuple-element.21), channel_id=1, source_target_pairs={{1008,1023},{1009,1010},{1010,1009},{1011,1012},{1012,1011},{1013,... | collective-permute-start | bytes 325640 | tf_op jit(solution)/shard_map/ppermute | solution.py:274
  90.7 24.0 %collective-permute-start.13 = (f32[53,1,128]{2,1,0:T(1,128)S(1)}, f32[53,1,128]{2,1,0:T(1,128)S(1)}, u32[]{:S(2)}, u32[]{:S(2)}) collective-permute-start(f32[53,1,128]{2,1,0:T(1,128)S(1)} %edge_1.1), channel_id=1, source_target_pairs={{2,3},{3,2},{6,7},{7,6},{10,11},{11,10},{14,15},{15,14},{1008,1009... | collective-permute-start | bytes 81416 | tf_op jit(solution)/shard_map/ppermute | solution.py:307
  91.4 23.3 %collective-permute-start.12 = (f32[53,1,128]{2,1,0:T(1,128)S(1)}, f32[53,1,128]{2,1,0:T(1,128)S(1)}, u32[]{:S(2)}, u32[]{:S(2)}) collective-permute-start(f32[53,1,128]{2,1,0:T(1,128)S(1)} %edge_0.1), channel_id=1, source_target_pairs={{0,1},{1,0},{4,5},{5,4},{8,9},{9,8},{12,13},{13,12}} | collective-permute-start | bytes 81416 | tf_op jit(solution)/shard_map/ppermute | solution.py:299
where the time goes:
time: 123 us
  waiting for transfers between devices  61.3 us (50%)
  starting transfers between devices  48.7 us (40%)
  Pallas kernels  9.44 us (8%)
  local copies, waits for them, and re-layouts  2.35 us (2%)
    ppermute x1, starting transfers between devices, shards(): lax.ppermute(x, both, [(at(i + 1, j), at(i, j)) for i, j in others] + [(a...  29 us
    ppermute x3, waiting for transfers between devices, long_swap(): lax.ppermute(long_msg, both, [(at(i, j), at(i, partner[j])) for i, j in s...  20.5 us
    ppermute x1, waiting for transfers between devices, shards(): lax.ppermute(down_msg, both, [(at(0, j), at(end, partner[j])) for j in ea...  16.4 us
    ppermute x1, waiting for transfers between devices, shards(): lax.ppermute(up_msg, both, [(at(end, partner[j]), at(0, j)) for j in early])  12.2 us
    ppermute x1, waiting for transfers between devices, shards(): lax.ppermute(down_msg, both, [(at(a, j), at(b, j)) for a, b in down for j...  12.1 us
    pallas_call x1, Pallas kernels, shards(): pl.pallas_call(final_kernel, out_shape=sds(S * 16, H), in_specs=[SM, SM]...  8 us
    ppermute x3, starting transfers between devices, long_swap(): lax.ppermute(long_msg, both, [(at(i, j), at(i, partner[j])) for i, j in s...  6.05 us
  transfers between devices with their start and end apart: 14, of which 4 were waited for; matrix products, arithmetic and copies ran while one was open for 2% of the time, Pallas kernels for 1%

commit v1 on v0

--- a/solution.py
+++ b/solution.py
@@ -18,44 +18,44 @@
 SM = pl.BlockSpec(memory_space=pltpu.SMEM)
 
 
+def column(ref, row, col):
+    return ref[pl.ds(8 * row + col, S, stride=16), :]
+
+
 def pack_kernel(x, long_out, short_out, up_out, down_out):
     p = lax.axis_index("narrow") % 2
     long_near = jnp.where(p == 0, 0, 7)
     long_far = jnp.where(p == 0, 1, 6)
-    short_near = 7 - long_near
-    short_far = 7 - long_far
     for r, row_out in ((0, down_out), (1, up_out)):
-        long_edge = x[:, r, pl.ds(long_near, 1), :]
-        short_edge = x[:, r, pl.ds(short_near, 1), :]
-        long_out[:, r : r + 1, :] = long_edge
-        short_out[:, r : r + 1, :] = short_edge
-        row_out[:, 0:1, :] = long_edge
-        row_out[:, 1:2, :] = short_edge
-        long_out[:, 2 + r : 3 + r, :] = x[:, r, pl.ds(long_far, 1), :]
-        short_out[:, 2 + r : 3 + r, :] = x[:, r, pl.ds(short_far, 1), :]
+        long_edge = column(x, r, long_near)
+        short_edge = column(x, r, 7 - long_near)
+        long_out[r] = long_edge
+        short_out[r] = short_edge
+        row_out[0] = long_edge
+        row_out[1] = short_edge
+        long_out[2 + r] = column(x, r, long_far)
+        short_out[2 + r] = column(x, r, 7 - long_far)
 
 
 def fold_kernel(long, short, below, above, long_out, short_out):
-    long_out[:, 0:2, :] = long[:, 0:2, :]
-    short_out[:, 0:2, :] = short[:, 0:2, :]
     w = lax.axis_index("wide")
     low = jnp.where(w == 0, 0.0, 2.0)
     high = jnp.where(w == lax.axis_size("wide") - 1, 0.0, 2.0)
-    long_out[:, 2:3, :] = long[:, 2:3, :] + low * below[:, 0:1, :]
-    long_out[:, 3:4, :] = long[:, 3:4, :] + high * above[:, 0:1, :]
-    short_out[:, 2:3, :] = short[:, 2:3, :] + low * below[:, 1:2, :]
-    short_out[:, 3:4, :] = short[:, 3:4, :] + high * above[:, 1:2, :]
+    for k, got, out in ((0, long, long_out), (1, short, short_out)):
+        out[0:2] = got[0:2]
+        out[2] = got[2] + low * below[k]
+        out[3] = got[3] + high * above[k]
 
 
 def first_edge_kernel(up, out):
     at = jnp.where(lax.axis_index("narrow") % 2 == 0, 7, 0)
-    out[...] = up[:, 1, pl.ds(at, 1), :]
+    out[...] = column(up, 1, at)
 
 
 def edge_kernel(up, down, out):
     at = jnp.where(lax.axis_index("narrow") % 2 == 0, 7, 0)
     first = lax.axis_index("wide") == 0
-    out[...] = jnp.where(first, up[:, 1, pl.ds(at, 1), :], down[:, 0, pl.ds(at, 1), :])
+    out[...] = jnp.where(first, column(up, 1, at), column(down, 0, at))
 
 
 def around(v):
@@ -81,6 +81,7 @@
     corner_0,
     corner_1,
     temps,
+    spread_column,
     rate,
     left,
     right,
@@ -97,51 +98,55 @@
     sub = lax.broadcasted_iota(jnp.int32, (8, H), 0)
     is_lo = sub == 0
     is_hi = sub == 7
-    long_edge = jnp.where(even, 0, 7)
-    long_first = sub == jnp.where(at_first, long_edge, 8)
-    long_last = sub == jnp.where(at_last, long_edge, 8)
-    short_first = sub == jnp.where(at_first, 7 - long_edge, 8)
-    short_last = sub == jnp.where(at_last, 7 - long_edge, 8)
-
-    def beside(v, lo, hi):
-        down = jnp.where(is_lo, lo, pltpu.roll(v, 1, 0))
-        up = jnp.where(is_hi, hi, pltpu.roll(v, 7, 0))
+
+    def beside(v):
+        down = jnp.where(is_lo, 0.0, pltpu.roll(v, 1, 0))
+        up = jnp.where(is_hi, 0.0, pltpu.roll(v, 7, 0))
         return down + up
 
     for s in range(S):
         c = spread[s]
-        v0 = x[s, 0]
-        v1 = x[s, 1]
-        below_rows = up_0[s] + up_1[s]
-        above_rows = down_0[s] + down_1[s]
-        below_far = below_rows[0]
-        below = below_rows[1]
-        above = above_rows[0]
-        above_far = above_rows[1]
-        near_corner = 2.0 * (corner_0[s] + corner_1[s])
-        below_far = below_far + jnp.where(long_first, 2.0 * (diag_below[s, 0:1, :] + across_a[s, 0:1, :]), 0.0)
-        above_far = above_far + jnp.where(long_last, 2.0 * (diag_above[s, 0:1, :] + across_b[s, 0:1, :]), 0.0)
-        below_far = below_far + jnp.where(short_first, near_corner, 0.0)
-        above_far = above_far + jnp.where(short_last, near_corner, 0.0)
-        long_s = long_d[s] + long_b[s] + long_c[s]
-        lo = jnp.where(even, long_s, short[s])
-        hi = jnp.where(even, short[s], long_s)
-        u_lo = []
-        u_hi = []
+        keep = 1.0 - 6.0 * c
+        at = 16 * s
+        v0 = x[at : at + 8, :]
+        v1 = x[at + 8 : at + 16, :]
+        below_far = up_0[s, 0] + up_1[s, 0]
+        below = up_0[s, 1] + up_1[s, 1]
+        above = down_0[s, 0] + down_1[s, 0]
+        above_far = down_0[s, 1] + down_1[s, 1]
+        u0 = keep * v0 + c * (below + v1 + beside(v0) + around(v0))
+        u1 = keep * v1 + c * (v0 + above + beside(v1) + around(v1))
+        t0 = u0 + c * below
+        t1 = u1 + c * above
+        n0 = keep * below + c * (below_far + v0) + u1 + beside(t0) + around(t0)
+        n1 = keep * above + c * (above_far + v1) + u0 + beside(t1) + around(t1)
+        out[at : at + 8, :] = keep * u0 + c * n0
+        out[at + 8 : at + 16, :] = keep * u1 + c * n1
+
+    c = spread_column[...]
+    c2 = c * c
+    once = 2.0 * c * (1.0 - 6.0 * c)
+    long_edge = jnp.where(even, 0, 7)
+    low = jnp.where(at_first, 2.0, 0.0)
+    high = jnp.where(at_last, 2.0, 0.0)
+    long = [long_d[k] + long_b[k] + long_c[k] for k in range(4)]
+    ends_long = (low * (diag_below[0] + across_a[0]), high * (diag_above[0] + across_b[0]))
+    near_corner = corner_0[...] + corner_1[...]
+    ends_short = (low * near_corner, high * near_corner)
+    for got, ends, edge in (
+        (long, ends_long, long_edge),
+        ([short[k] for k in range(4)], ends_short, 7 - long_edge),
+    ):
+        inner = jnp.where(edge == 0, 1, 6)
         for r in range(2):
-            v = (v0, v1)[r]
-            for side, edge, got in ((lo, 0, u_lo), (hi, 7, u_hi)):
-                near = side[r : r + 1]
-                n = side[2 + r : 3 + r] + side[1 - r : 2 - r] + v[edge : edge + 1] + around(near)
-                got.append(near + c * (n - 6.0 * near))
-        u0 = v0 + c * (below + v1 + beside(v0, lo[0:1], hi[0:1]) + around(v0) - 6.0 * v0)
-        u1 = v1 + c * (v0 + above + beside(v1, lo[1:2], hi[1:2]) + around(v1) - 6.0 * v1)
-        ub = below + c * (below_far + v0 + beside(below, 0.0, 0.0) + around(below) - 6.0 * below)
-        ua = above + c * (above_far + v1 + beside(above, 0.0, 0.0) + around(above) - 6.0 * above)
-        m0 = u0 + c * (ub + u1 + beside(u0, u_lo[0], u_hi[0]) + around(u0) - 6.0 * u0)
-        m1 = u1 + c * (u0 + ua + beside(u1, u_lo[1], u_hi[1]) + around(u1) - 6.0 * u1)
-        out[16 * s : 16 * s + 8, :] = m0
-        out[16 * s + 8 : 16 * s + 16, :] = m1
+            near = got[r]
+            add = once * near + c2 * (
+                2.0 * (around(near) + got[1 - r]) + got[2 + r] + ends[r] + column(x, r, edge)
+            )
+            spot = pl.ds(8 * r + edge, S, stride=16)
+            out[spot, :] = out[spot, :] + add
+            spot = pl.ds(8 * r + inner, S, stride=16)
+            out[spot, :] = out[spot, :] + c2 * near
 
     count = 0
     for col in range(16):
@@ -243,11 +248,11 @@
     down_0 = lax.ppermute(x, both, [(at(i + 1, j), at(i, j)) for i, j in first_half])
     long_raw, short_raw, up_msg, down_msg = pl.pallas_call(
         pack_kernel,
-        out_shape=(vds(S, 4, H), vds(S, 4, H), vds(S, 2, H), vds(S, 2, H)),
+        out_shape=(vds(4, S, H), vds(4, S, H), vds(2, S, H), vds(2, S, H)),
         in_specs=[VM],
         out_specs=(VM,) * 4,
         name="pack",
-    )(x)
+    )(x.reshape(S * 16, H))
     corner_below = lax.ppermute(
         up_msg,
         both,
@@ -264,7 +269,7 @@
     across_b = lax.ppermute(down_msg, both, [(at(0, j), at(end, partner[j])) for j in early])
     long_msg, short_msg = pl.pallas_call(
         fold_kernel,
-        out_shape=(vds(S, 4, H), vds(S, 4, H)),
+        out_shape=(vds(4, S, H), vds(4, S, H)),
         in_specs=[VM] * 4,
         out_specs=(VM,) * 2,
         name="fold",
@@ -285,25 +290,28 @@
         [(at(i + 1, j), at(i, j)) for i, j in others]
         + [(at(0, j), at(end, j)) for j in range(nn)],
     )
-    short_msg, left, right, rate = lax.optimization_barrier((short_msg, left, right, rate))
+    spread_column = spreading_number[:, None]
+    short_msg, left, right, rate, spread_column = lax.optimization_barrier(
+        (short_msg, left, right, rate, spread_column)
+    )
     short = lax.ppermute(short_msg, "narrow", [(j, j ^ 1) for j in range(nn)])
     long_c = long_swap([(0, j) for j in early])
     long_d = long_swap([(end, j) for j in range(nn)])
     edge_0 = pl.pallas_call(
         first_edge_kernel,
-        out_shape=vds(S, 1, H),
+        out_shape=vds(S, H),
         in_specs=[VM],
         out_specs=VM,
         name="edge_0",
-    )(vmem(up_0))
+    )(vmem(up_0.reshape(S * 16, H)))
     corner_0 = lax.ppermute(edge_0, both, [(at(0, j), at(0, j ^ 1)) for j in early])
     edge_1 = pl.pallas_call(
         edge_kernel,
-        out_shape=vds(S, 1, H),
+        out_shape=vds(S, H),
         in_specs=[VM] * 2,
         out_specs=VM,
         name="edge_1",
-    )(vmem(up_1), vmem(down_1))
+    )(vmem(up_1.reshape(S * 16, H)), vmem(down_1.reshape(S * 16, H)))
     corner_1 = lax.ppermute(
         edge_1,
         both,
@@ -313,14 +321,14 @@
     out = pl.pallas_call(
         final_kernel,
         out_shape=sds(S * 16, H),
-        in_specs=[SM, SM] + [VM] * 19,
+        in_specs=[SM, SM] + [VM] * 20,
         out_specs=VM,
         scratch_shapes=[pltpu.SMEM((17,), jnp.int32), pltpu.VMEM((3 * SP, BURN_MAX * H), bf)],
         name="step",
     )(
         ignited_stacks,
         spreading_number,
-        x,
+        x.reshape(S * 16, H),
         vmem(up_0),
         vmem(up_1),
         vmem(down_0),
@@ -336,6 +344,7 @@
         vmem(corner_0),
         vmem(corner_1),
         thermal_state.reshape(16, H),
+        spread_column,
         rate,
         left,
         right,

time: 123 us -> 120 us (0.976)
  waiting for transfers between devices: 61.3 us -> 37.5 us
  starting transfers between devices: 48.7 us -> 69.1 us
    ppermute x3, starting transfers between devices: 6.05 us -> 26.7 us  [long_swap(): lax.ppermute(long_msg, both, [(at(i, j), at(i, partner[j])) for i, j in s...]
    ppermute x1, waiting for transfers between devices: 16.4 us -> 0.94 us  [shards(): lax.ppermute(down_msg, both, [(at(0, j), at(end, partner[j])) for j in ea...]
    ppermute x1, waiting for transfers between devices: 12.2 us -> 7.06 us  [shards(): lax.ppermute(up_msg, both, [(at(end, partner[j]), at(0, j)) for j in early])]
    ppermute x1, waiting for transfers between devices: 12.1 us -> 9.87 us  [shards(): lax.ppermute(down_msg, both, [(at(a, j), at(b, j)) for a, b in down for j...]
    ppermute x1, starting transfers between devices: 29 us -> 27.3 us  [shards(): lax.ppermute(x, both, [(at(i + 1, j), at(i, j)) for i, j in others] + [(a...]
    ppermute x1, starting transfers between devices: 1.92 us -> 3.49 us  [shards(): lax.ppermute(x, both, [(at(i, j), at(i + 1, j)) for i, j in first_half] +...]
  transfers between devices with their start and end apart: 14 -> 14, of which waited for: 4 -> 4; matrix products, arithmetic and copies ran while one was open for 2% -> 3% of each run, Pallas kernels for 1% -> 1%
where the time goes in v1:
time: 120 us; the launch traced here: 119 us
  starting transfers between devices  69.1 us (58%)
  waiting for transfers between devices  37.5 us (31%)
  Pallas kernels  8.78 us (7%)
  local copies, waits for them, and re-layouts  3.04 us (3%)
    ppermute x1, starting transfers between devices, shards(): lax.ppermute(x, both, [(at(i + 1, j), at(i, j)) for i, j in others] + [(a...  27.3 us
    ppermute x3, starting transfers between devices, long_swap(): lax.ppermute(long_msg, both, [(at(i, j), at(i, partner[j])) for i, j in s...  26.7 us
    ppermute x3, waiting for transfers between devices, long_swap(): lax.ppermute(long_msg, both, [(at(i, j), at(i, partner[j])) for i, j in s...  19.6 us
    ppermute x1, waiting for transfers between devices, shards(): lax.ppermute(down_msg, both, [(at(a, j), at(b, j)) for a, b in down for j...  9.87 us
    pallas_call x1, Pallas kernels, shards(): pl.pallas_call(final_kernel, out_shape=sds(S * 16, H), in_specs=[SM, SM]...  7.54 us
    ppermute x1, waiting for transfers between devices, shards(): lax.ppermute(up_msg, both, [(at(end, partner[j]), at(0, j)) for j in early])  7.06 us
    ppermute x1, starting transfers between devices, shards(): lax.ppermute(x, both, [(at(i, j), at(i + 1, j)) for i, j in first_half] +...  3.49 us
  transfers between devices with their start and end apart: 14, of which 4 were waited for; matrix products, arithmetic and copies ran while one was open for 3% of the time, Pallas kernels for 1%

profile of v1, /device:TPU:6, one launch (start us, length us, event | category | flops | bytes accessed | tf_op | source)
XLA Modules:
  0.0 119.5 jit_solution(5827672149841308993)
XLA Ops:
  0.0 0.7 collective-permute-start.1
  0.7 3.5 %collective-permute-start = (f32[53,2,8,128]{3,2,1,0:T(8,128)}, f32[53,2,8,128]{3,2,1,0:T(8,128)S(1)}, u32[]{:S(2)}, u32[]{:S(2)}) collective-permute-start(f32[53,2,8,128]{3,2,1,0:T(8,128)} %param.8), channel_id=1, source_target_pairs={{0,16},{1,17},{4,20},{5,21},{8,24},{9,25},{12,28},{13,29},{16,32},... | collective-permute-start | bytes 1302536 | tf_op jit(solution)/shard_map/ppermute | solution.py:242
  4.2 27.3 %collective-permute-start.3 = (f32[53,2,8,128]{3,2,1,0:T(8,128)}, f32[53,2,8,128]{3,2,1,0:T(8,128)S(1)}, u32[]{:S(2)}, u32[]{:S(2)}) collective-permute-start(f32[53,2,8,128]{3,2,1,0:T(8,128)} %param.8), channel_id=1, source_target_pairs={{18,2},{19,3},{22,6},{23,7},{26,10},{27,11},{30,14},{31,15},{34,18... | collective-permute-start | bytes 1302536 | tf_op jit(solution)/shard_map/ppermute | solution.py:287
  31.5 0.0 copy-start
  31.5 1.1 pack.1
  32.7 1.3 %collective-permute-start.10 = (f32[2,53,128]{2,1,0:T(8,128)S(1)}, f32[2,53,128]{2,1,0:T(8,128)S(1)}, u32[]{:S(2)}, u32[]{:S(2)}) collective-permute-start(f32[2,53,128]{2,1,0:T(8,128)S(1)} %get-tuple-element.18), channel_id=1, source_target_pairs={{1023,0},{1010,1},{1011,4},{1014,5},{1015,8},{1018,9},{1019,12},{1... | collective-permute-start | bytes 162824 | tf_op jit(solution)/shard_map/ppermute | solution.py:268
  34.0 1.3 %collective-permute-start.4 = (f32[2,53,128]{2,1,0:T(8,128)S(1)}, f32[2,53,128]{2,1,0:T(8,128)S(1)}, u32[]{:S(2)}, u32[]{:S(2)}) collective-permute-start(f32[2,53,128]{2,1,0:T(8,128)S(1)} %get-tuple-element.18), channel_id=1, source_target_pairs={{0,16},{1,17},{2,18},{3,19},{4,20},{5,21},{6,22},{7,23},{8,24},{9,... | collective-permute-start | bytes 162824 | tf_op jit(solution)/shard_map/ppermute | solution.py:256
  35.3 0.0 copy-done
  35.3 0.0 copy-start.1
  35.3 7.1 %collective-permute-done.10.across_a = f32[2,53,128]{2,1,0:T(8,128)S(1)} collective-permute-done((f32[2,53,128]{2,1,0:T(8,128)S(1)}, f32[2,53,128]{2,1,0:T(8,128)S(1)}, u32[]{:S(2)}, u32[]{:S(2)}) %collective-permute-start.10) | collective-permute-done | bytes 54304 | tf_op jit(solution)/shard_map/ppermute | solution.py:268
  42.4 1.3 %collective-permute-start.2 = (f32[53,2,8,128]{3,2,1,0:T(8,128)}, f32[53,2,8,128]{3,2,1,0:T(8,128)S(1)}, u32[]{:S(2)}, u32[]{:S(2)}) collective-permute-start(f32[53,2,8,128]{3,2,1,0:T(8,128)} %param.8), channel_id=1, source_target_pairs={{16,0},{17,1},{20,4},{21,5},{24,8},{25,9},{28,12},{29,13},{32,16},... | collective-permute-start | bytes 1302536 | tf_op jit(solution)/shard_map/ppermute | solution.py:248
  43.7 0.0 copy-done.1
  43.7 0.0 collective-permute-done.4.below.diag_below
  43.7 0.0 copy-start.2
  43.7 1.3 %collective-permute-start.5 = (f32[2,53,128]{2,1,0:T(8,128)S(1)}, f32[2,53,128]{2,1,0:T(8,128)S(1)}, u32[]{:S(2)}, u32[]{:S(2)}) collective-permute-start(f32[2,53,128]{2,1,0:T(8,128)S(1)} %get-tuple-element.19), channel_id=1, source_target_pairs={{16,0},{17,1},{18,2},{19,3},{20,4},{21,5},{22,6},{23,7},{24,8},{25... | collective-permute-start | bytes 162824 | tf_op jit(solution)/shard_map/ppermute | solution.py:262
  45.0 0.7 fusion.2.right
  45.7 0.0 copy-done.2
  45.7 0.0 copy-start.3
  45.7 0.7 copy-done.3
  46.4 9.9 %collective-permute-done.5.above.diag_above = f32[2,53,128]{2,1,0:T(8,128)S(1)} collective-permute-done((f32[2,53,128]{2,1,0:T(8,128)S(1)}, f32[2,53,128]{2,1,0:T(8,128)S(1)}, u32[]{:S(2)}, u32[]{:S(2)}) %collective-permute-start.5) | collective-permute-done | bytes 54304 | tf_op jit(solution)/shard_map/ppermute | solution.py:262
  56.3 1.3 %collective-permute-start.11 = (f32[2,53,128]{2,1,0:T(8,128)S(1)}, f32[2,53,128]{2,1,0:T(8,128)S(1)}, u32[]{:S(2)}, u32[]{:S(2)}) collective-permute-start(f32[2,53,128]{2,1,0:T(8,128)S(1)} %get-tuple-element.19), channel_id=1, source_target_pairs={{0,1023},{1,1010},{4,1011},{5,1014},{8,1015},{9,1018},{12,1019},{1... | collective-permute-start | bytes 162824 | tf_op jit(solution)/shard_map/ppermute | solution.py:269
  57.6 0.1 copy.15
  57.7 0.7 pad.13.rate
  58.4 0.9 collective-permute-done.11.across_b
  59.3 1.9 %collective-permute-start.6 = (f32[4,53,128]{2,1,0:T(8,128)S(1)}, f32[4,53,128]{2,1,0:T(8,128)S(1)}, u32[]{:S(2)}, u32[]{:S(2)}) collective-permute-start(f32[4,53,128]{2,1,0:T(8,128)S(1)} %get-tuple-element.21), channel_id=1, source_target_pairs={{0,1},{1,0},{2,3},{3,2},{4,5},{5,4},{6,7},{7,6},{8,9},{9,8},{10,11... | collective-permute-start | bytes 325640 | tf_op jit(solution)/shard_map/ppermute | solution.py:297
  61.3 0.0 collective-permute-done.1.up_1
  61.3 24.7 %collective-permute-start.9 = (f32[4,53,128]{2,1,0:T(8,128)S(1)}, f32[4,53,128]{2,1,0:T(8,128)S(1)}, u32[]{:S(2)}, u32[]{:S(2)}) collective-permute-start(f32[4,53,128]{2,1,0:T(8,128)S(1)} %get-tuple-element.22), channel_id=1, source_target_pairs={{0,15},{1,2},{4,3},{5,6},{8,7},{9,10},{12,11},{13,14}} | collective-permute-start | bytes 325640 | tf_op jit(solution)/shard_map/ppermute | solution.py:279
  86.0 0.0 collective-permute-done.up_0
  86.0 1.3 %collective-permute-start.8 = (f32[4,53,128]{2,1,0:T(8,128)S(1)}, f32[4,53,128]{2,1,0:T(8,128)S(1)}, u32[]{:S(2)}, u32[]{:S(2)}) collective-permute-start(f32[4,53,128]{2,1,0:T(8,128)S(1)} %get-tuple-element.22), channel_id=1, source_target_pairs={{2,1},{3,4},{6,5},{7,8},{10,9},{11,12},{14,13},{15,0},{16,31},{17,... | collective-permute-start | bytes 325640 | tf_op jit(solution)/shard_map/ppermute | solution.py:279
  87.3 0.0 collective-permute-done.3.down_1
  87.4 0.7 collective-permute-start.7
  88.1 0.0 copy-start.4
  88.1 0.0 collective-permute-done.6.short
  88.1 1.9 %collective-permute-start.12 = (f32[53,128]{1,0:T(8,128)S(1)}, f32[53,128]{1,0:T(8,128)S(1)}, u32[]{:S(2)}, u32[]{:S(2)}) collective-permute-start(f32[53,128]{1,0:T(8,128)S(1)} %edge_0.1), channel_id=1, source_target_pairs={{0,1},{1,0},{4,5},{5,4},{8,9},{9,8},{12,13},{13,12}} | collective-permute-start | bytes 81416 | tf_op jit(solution)/shard_map/ppermute | solution.py:307
  90.1 0.0 collective-permute-done.9.long_c
  90.1 0.7 collective-permute-start.13
  90.7 0.0 copy-done.4
  90.8 0.7 copy.16.spread_column
  91.5 0.8 copy.17.left
  92.3 19.6 %collective-permute-done.8.long_b = f32[4,53,128]{2,1,0:T(8,128)S(1)} collective-permute-done((f32[4,53,128]{2,1,0:T(8,128)S(1)}, f32[4,53,128]{2,1,0:T(8,128)S(1)}, u32[]{:S(2)}, u32[]{:S(2)}) %collective-permute-start.8) | collective-permute-done | bytes 108576 | tf_op jit(solution)/shard_map/ppermute | solution.py:279
  111.9 0.0 collective-permute-done.7.long_d
  111.9 0.0 collective-permute-done.2.down_0
  111.9 0.0 collective-permute-done.12.corner_0
  111.9 0.0 collective-permute-done.13.corner_1
  111.9 7.5 %step.1 = f32[848,128]{1,0:T(8,128)} custom-call(s32[2,8]{1,0:T(2,128)} %marks.1, f32[53]{0:T(128)} %spread.1, f32[848,128]{1,0:T(8,128)} %bitcast.x, f32[53,2,8,128]{3,2,1,0:T(8,128)S(1)} %collective-permute-done.up_0, f32[53,2,8,128]{3,2,1,0:T(8,128)S(1)} %collective-permute-done.1.up_1, f32[53,2,8,128]{3,2,1,0:T(8,128)S(1)} %collective-permute-done.2.down_0, ...), custom_call_target="tpu_custom_call" | custom-call | tf_op jit(solution)/shard_map/step/pallas_call | solution.py:321
  (10 shorter events, 0.2 us)
Async XLA Ops:
  0.0 61.3 %collective-permute-start.1 = (f32[53,2,8,128]{3,2,1,0:T(8,128)}, f32[53,2,8,128]{3,2,1,0:T(8,128)S(1)}, u32[]{:S(2)}, u32[]{:S(2)}) collective-permute-start(f32[53,2,8,128]{3,2,1,0:T(8,128)} %param.8), channel_id=1, source_target_pairs={{2,18},{3,19},{6,22},{7,23},{10,26},{11,27},{14,30},{15,31},{18,34... | collective-permute-start | bytes 1302536 | tf_op jit(solution)/shard_map/ppermute | solution.py:282
  0.7 85.3 %collective-permute-start = (f32[53,2,8,128]{3,2,1,0:T(8,128)}, f32[53,2,8,128]{3,2,1,0:T(8,128)S(1)}, u32[]{:S(2)}, u32[]{:S(2)}) collective-permute-start(f32[53,2,8,128]{3,2,1,0:T(8,128)} %param.8), channel_id=1, source_target_pairs={{0,16},{1,17},{4,20},{5,21},{8,24},{9,25},{12,28},{13,29},{16,32},... | collective-permute-start | bytes 1302536 | tf_op jit(solution)/shard_map/ppermute | solution.py:242
  4.2 83.2 %collective-permute-start.3 = (f32[53,2,8,128]{3,2,1,0:T(8,128)}, f32[53,2,8,128]{3,2,1,0:T(8,128)S(1)}, u32[]{:S(2)}, u32[]{:S(2)}) collective-permute-start(f32[53,2,8,128]{3,2,1,0:T(8,128)} %param.8), channel_id=1, source_target_pairs={{18,2},{19,3},{22,6},{23,7},{26,10},{27,11},{30,14},{31,15},{34,18... | collective-permute-start | bytes 1302536 | tf_op jit(solution)/shard_map/ppermute | solution.py:287
  31.5 3.8 %copy-start = (s32[325,53]{0,1:T(8,128)S(1)}, s32[325,53]{0,1:T(8,128)}, u32[]{:S(2)}) copy-start(s32[325,53]{0,1:T(8,128)} %param.14) | copy-start | bytes 206704
  32.7 9.7 %collective-permute-start.10 = (f32[2,53,128]{2,1,0:T(8,128)S(1)}, f32[2,53,128]{2,1,0:T(8,128)S(1)}, u32[]{:S(2)}, u32[]{:S(2)}) collective-permute-start(f32[2,53,128]{2,1,0:T(8,128)S(1)} %get-tuple-element.18), channel_id=1, source_target_pairs={{1023,0},{1010,1},{1011,4},{1014,5},{1015,8},{1018,9},{1019,12},{1... | collective-permute-start | bytes 162824 | tf_op jit(solution)/shard_map/ppermute | solution.py:268
  34.0 9.8 %collective-permute-start.4 = (f32[2,53,128]{2,1,0:T(8,128)S(1)}, f32[2,53,128]{2,1,0:T(8,128)S(1)}, u32[]{:S(2)}, u32[]{:S(2)}) collective-permute-start(f32[2,53,128]{2,1,0:T(8,128)S(1)} %get-tuple-element.18), channel_id=1, source_target_pairs={{0,16},{1,17},{2,18},{3,19},{4,20},{5,21},{6,22},{7,23},{8,24},{9,... | collective-permute-start | bytes 162824 | tf_op jit(solution)/shard_map/ppermute | solution.py:256
  35.3 8.4 %copy-start.1 = (s32[325,53]{0,1:T(8,128)S(1)}, s32[325,53]{0,1:T(8,128)}, u32[]{:S(2)}) copy-start(s32[325,53]{0,1:T(8,128)} %param.15) | copy-start | bytes 206704
  42.4 69.5 %collective-permute-start.2 = (f32[53,2,8,128]{3,2,1,0:T(8,128)}, f32[53,2,8,128]{3,2,1,0:T(8,128)S(1)}, u32[]{:S(2)}, u32[]{:S(2)}) collective-permute-start(f32[53,2,8,128]{3,2,1,0:T(8,128)} %param.8), channel_id=1, source_target_pairs={{16,0},{17,1},{20,4},{21,5},{24,8},{25,9},{28,12},{29,13},{32,16},... | collective-permute-start | bytes 1302536 | tf_op jit(solution)/shard_map/ppermute | solution.py:248
  43.7 2.0 %copy-start.2 = (f32[325]{0:T(512)S(1)}, f32[325]{0:T(512)}, u32[]{:S(2)}) copy-start(f32[325]{0:T(512)} %param.12) | copy-start | bytes 3904
  43.7 12.5 %collective-permute-start.5 = (f32[2,53,128]{2,1,0:T(8,128)S(1)}, f32[2,53,128]{2,1,0:T(8,128)S(1)}, u32[]{:S(2)}, u32[]{:S(2)}) collective-permute-start(f32[2,53,128]{2,1,0:T(8,128)S(1)} %get-tuple-element.19), channel_id=1, source_target_pairs={{16,0},{17,1},{18,2},{19,3},{20,4},{21,5},{22,6},{23,7},{24,8},{25... | collective-permute-start | bytes 162824 | tf_op jit(solution)/shard_map/ppermute | solution.py:262
  45.7 0.7 copy-start.3
  56.3 3.1 %collective-permute-start.11 = (f32[2,53,128]{2,1,0:T(8,128)S(1)}, f32[2,53,128]{2,1,0:T(8,128)S(1)}, u32[]{:S(2)}, u32[]{:S(2)}) collective-permute-start(f32[2,53,128]{2,1,0:T(8,128)S(1)} %get-tuple-element.19), channel_id=1, source_target_pairs={{0,1023},{1,1010},{4,1011},{5,1014},{8,1015},{9,1018},{12,1019},{1... | collective-permute-start | bytes 162824 | tf_op jit(solution)/shard_map/ppermute | solution.py:269
  59.3 28.8 %collective-permute-start.6 = (f32[4,53,128]{2,1,0:T(8,128)S(1)}, f32[4,53,128]{2,1,0:T(8,128)S(1)}, u32[]{:S(2)}, u32[]{:S(2)}) collective-permute-start(f32[4,53,128]{2,1,0:T(8,128)S(1)} %get-tuple-element.21), channel_id=1, source_target_pairs={{0,1},{1,0},{2,3},{3,2},{4,5},{5,4},{6,7},{7,6},{8,9},{9,8},{10,11... | collective-permute-start | bytes 325640 | tf_op jit(solution)/shard_map/ppermute | solution.py:297
  61.3 28.8 %collective-permute-start.9 = (f32[4,53,128]{2,1,0:T(8,128)S(1)}, f32[4,53,128]{2,1,0:T(8,128)S(1)}, u32[]{:S(2)}, u32[]{:S(2)}) collective-permute-start(f32[4,53,128]{2,1,0:T(8,128)S(1)} %get-tuple-element.22), channel_id=1, source_target_pairs={{0,15},{1,2},{4,3},{5,6},{8,7},{9,10},{12,11},{13,14}} | collective-permute-start | bytes 325640 | tf_op jit(solution)/shard_map/ppermute | solution.py:279
  86.0 25.9 %collective-permute-start.8 = (f32[4,53,128]{2,1,0:T(8,128)S(1)}, f32[4,53,128]{2,1,0:T(8,128)S(1)}, u32[]{:S(2)}, u32[]{:S(2)}) collective-permute-start(f32[4,53,128]{2,1,0:T(8,128)S(1)} %get-tuple-element.22), channel_id=1, source_target_pairs={{2,1},{3,4},{6,5},{7,8},{10,9},{11,12},{14,13},{15,0},{16,31},{17,... | collective-permute-start | bytes 325640 | tf_op jit(solution)/shard_map/ppermute | solution.py:279
  87.4 24.6 %collective-permute-start.7 = (f32[4,53,128]{2,1,0:T(8,128)S(1)}, f32[4,53,128]{2,1,0:T(8,128)S(1)}, u32[]{:S(2)}, u32[]{:S(2)}) collective-permute-start(f32[4,53,128]{2,1,0:T(8,128)S(1)} %get-tuple-element.22), channel_id=1, source_target_pairs={{1008,1023},{1009,1010},{1010,1009},{1011,1012},{1012,1011},{1013,... | collective-permute-start | bytes 325640 | tf_op jit(solution)/shard_map/ppermute | solution.py:279
  88.1 2.7 %copy-start.4 = (f32[53]{0:T(128)S(1)}, f32[53]{0:T(128)}, u32[]{:S(2)}) copy-start(f32[53]{0:T(128)} %spread.1) | copy-start | bytes 640
  88.1 23.8 %collective-permute-start.12 = (f32[53,128]{1,0:T(8,128)S(1)}, f32[53,128]{1,0:T(8,128)S(1)}, u32[]{:S(2)}, u32[]{:S(2)}) collective-permute-start(f32[53,128]{1,0:T(8,128)S(1)} %edge_0.1), channel_id=1, source_target_pairs={{0,1},{1,0},{4,5},{5,4},{8,9},{9,8},{12,13},{13,12}} | collective-permute-start | bytes 81416 | tf_op jit(solution)/shard_map/ppermute | solution.py:307
  90.1 21.8 %collective-permute-start.13 = (f32[53,128]{1,0:T(8,128)S(1)}, f32[53,128]{1,0:T(8,128)S(1)}, u32[]{:S(2)}, u32[]{:S(2)}) collective-permute-start(f32[53,128]{1,0:T(8,128)S(1)} %edge_1.1), channel_id=1, source_target_pairs={{2,3},{3,2},{6,7},{7,6},{10,11},{11,10},{14,15},{15,14},{1008,1009... | collective-permute-start | bytes 81416 | tf_op jit(solution)/shard_map/ppermute | solution.py:315

commit v2 on v1

--- a/solution.py
+++ b/solution.py
@@ -56,6 +56,12 @@
     at = jnp.where(lax.axis_index("narrow") % 2 == 0, 7, 0)
     first = lax.axis_index("wide") == 0
     out[...] = jnp.where(first, column(up, 1, at), column(down, 0, at))
+
+
+def hold_kernel(left, right, rate, left_out, right_out, rate_out):
+    left_out[...] = left[...]
+    right_out[...] = right[...]
+    rate_out[...] = rate[...]
 
 
 def around(v):
@@ -81,13 +87,13 @@
     corner_0,
     corner_1,
     temps,
-    spread_column,
     rate,
     left,
     right,
     out,
     index,
     stack,
+    spread_column,
 ):
     w = lax.axis_index("wide")
     p = lax.axis_index("narrow") % 2
@@ -107,13 +113,16 @@
     for s in range(S):
         c = spread[s]
         keep = 1.0 - 6.0 * c
+        spread_column[s : s + 1, :] = jnp.full((1, H), c)
         at = 16 * s
         v0 = x[at : at + 8, :]
         v1 = x[at + 8 : at + 16, :]
-        below_far = up_0[s, 0] + up_1[s, 0]
-        below = up_0[s, 1] + up_1[s, 1]
-        above = down_0[s, 0] + down_1[s, 0]
-        above_far = down_0[s, 1] + down_1[s, 1]
+        far = pl.ds(at, 8)
+        near = pl.ds(at + 8, 8)
+        below_far = up_0[far, :] + up_1[far, :]
+        below = up_0[near, :] + up_1[near, :]
+        above = down_0[far, :] + down_1[far, :]
+        above_far = down_0[near, :] + down_1[near, :]
         u0 = keep * v0 + c * (below + v1 + beside(v0) + around(v0))
         u1 = keep * v1 + c * (v0 + above + beside(v1) + around(v1))
         t0 = u0 + c * below
@@ -290,20 +299,34 @@
         [(at(i + 1, j), at(i, j)) for i, j in others]
         + [(at(0, j), at(end, j)) for j in range(nn)],
     )
-    spread_column = spreading_number[:, None]
-    short_msg, left, right, rate, spread_column = lax.optimization_barrier(
-        (short_msg, left, right, rate, spread_column)
-    )
+    left, right, rate = pl.pallas_call(
+        hold_kernel,
+        out_shape=(
+            jax.ShapeDtypeStruct(left.shape, bf),
+            jax.ShapeDtypeStruct(right.shape, bf),
+            jax.ShapeDtypeStruct(rate.shape, jnp.float32),
+        ),
+        in_specs=[VM] * 3,
+        out_specs=(VM,) * 3,
+        name="hold",
+    )(left, right, rate)
+    short_msg, left, right, rate = lax.optimization_barrier((short_msg, left, right, rate))
     short = lax.ppermute(short_msg, "narrow", [(j, j ^ 1) for j in range(nn)])
     long_c = long_swap([(0, j) for j in early])
     long_d = long_swap([(end, j) for j in range(nn)])
+    rows = {id(v): v.reshape(S * 16, H) for v in (up_0, down_0)}
+    rows |= {id(v): vmem(v.reshape(S * 16, H)) for v in (up_1, down_1)}
+
+    def flat(value):
+        return rows[id(value)]
+
     edge_0 = pl.pallas_call(
         first_edge_kernel,
         out_shape=vds(S, H),
         in_specs=[VM],
         out_specs=VM,
         name="edge_0",
-    )(vmem(up_0.reshape(S * 16, H)))
+    )(flat(up_0))
     corner_0 = lax.ppermute(edge_0, both, [(at(0, j), at(0, j ^ 1)) for j in early])
     edge_1 = pl.pallas_call(
         edge_kernel,
@@ -311,7 +334,7 @@
         in_specs=[VM] * 2,
         out_specs=VM,
         name="edge_1",
-    )(vmem(up_1.reshape(S * 16, H)), vmem(down_1.reshape(S * 16, H)))
+    )(flat(up_1), flat(down_1))
     corner_1 = lax.ppermute(
         edge_1,
         both,
@@ -321,30 +344,29 @@
     out = pl.pallas_call(
         final_kernel,
         out_shape=sds(S * 16, H),
-        in_specs=[SM, SM] + [VM] * 20,
+        in_specs=[SM, SM] + [VM] * 19,
         out_specs=VM,
-        scratch_shapes=[pltpu.SMEM((17,), jnp.int32), pltpu.VMEM((3 * SP, BURN_MAX * H), bf)],
+        scratch_shapes=[pltpu.SMEM((17,), jnp.int32), pltpu.VMEM((3 * SP, BURN_MAX * H), bf), vds(S, H)],
         name="step",
     )(
         ignited_stacks,
         spreading_number,
         x.reshape(S * 16, H),
-        vmem(up_0),
-        vmem(up_1),
-        vmem(down_0),
-        vmem(down_1),
+        flat(up_0),
+        flat(up_1),
+        flat(down_0),
+        flat(down_1),
         vmem(short),
         vmem(long_d),
         vmem(long_b),
         vmem(long_c),
-        vmem(corner_below),
-        vmem(corner_above),
-        vmem(across_a),
-        vmem(across_b),
+        corner_below,
+        corner_above,
+        across_a,
+        across_b,
         vmem(corner_0),
         vmem(corner_1),
         thermal_state.reshape(16, H),
-        spread_column,
         rate,
         left,
         right,

time: 120 us -> 126 us (1.050)
  starting transfers between devices: 69.1 us -> 73 us
  Pallas kernels: 8.78 us -> 11.6 us
  waiting for transfers between devices: 37.5 us -> 35.6 us
    ppermute x3, starting transfers between devices: 26.7 us -> 30 us  [long_swap(): lax.ppermute(long_msg, both, [(at(i, j), at(i, partner[j])) for i, j in s...]
    pallas_call x0 -> x1, Pallas kernels: none -> 1.84 us  [shards(): pl.pallas_call(hold_kernel, out_shape=(jax.ShapeDtypeStruct(left.shape, b...]
    optimization_barrier x2 -> x0, local copies, waits for them, and re-layouts: 1.51 us -> none  [shards(): lax.optimization_barrier((short_msg, left, right, rate, spread_column))]
  transfers between devices with their start and end apart: 14 -> 14, of which waited for: 4 -> 3; matrix products, arithmetic and copies ran while one was open for 3% -> 3% of each run, Pallas kernels for 1% -> 3%
where the time goes in v2:
time: 126 us; the launch traced here: 125 us
  starting transfers between devices  73 us (58%)
  waiting for transfers between devices  35.6 us (28%)
  Pallas kernels  11.6 us (9%)
  local copies, waits for them, and re-layouts  3.11 us (2%)
  other arithmetic  1.58 us (1%)
    ppermute x3, starting transfers between devices, long_swap(): lax.ppermute(long_msg, both, [(at(i, j), at(i, partner[j])) for i, j in s...  30 us
    ppermute x1, starting transfers between devices, shards(): lax.ppermute(x, both, [(at(i + 1, j), at(i, j)) for i, j in others] + [(a...  27.3 us
    ppermute x3, waiting for transfers between devices, long_swap(): lax.ppermute(long_msg, both, [(at(i, j), at(i, partner[j])) for i, j in s...  19.9 us
    ppermute x1, waiting for transfers between devices, shards(): lax.ppermute(down_msg, both, [(at(a, j), at(b, j)) for a, b in down for j...  9.52 us
    pallas_call x1, Pallas kernels, shards(): pl.pallas_call(final_kernel, out_shape=sds(S * 16, H), in_specs=[SM, SM]...  7.58 us
    ppermute x1, waiting for transfers between devices, shards(): lax.ppermute(up_msg, both, [(at(end, partner[j]), at(0, j)) for j in early])  6.19 us
    ppermute x1, starting transfers between devices, shards(): lax.ppermute(x, both, [(at(i, j), at(i + 1, j)) for i, j in first_half] +...  3.49 us
  transfers between devices with their start and end apart: 14, of which 3 were waited for; matrix products, arithmetic and copies ran while one was open for 3% of the time, Pallas kernels for 3%

profile of v2, /device:TPU:6, one launch (start us, length us, event | category | flops | bytes accessed | tf_op | source)
XLA Modules:
  0.0 125.3 jit_solution(3577809461166035381)
XLA Ops:
  0.0 0.8 collective-permute-start.1
  0.8 3.5 %collective-permute-start = (f32[53,2,8,128]{3,2,1,0:T(8,128)}, f32[53,2,8,128]{3,2,1,0:T(8,128)S(1)}, u32[]{:S(2)}, u32[]{:S(2)}) collective-permute-start(f32[53,2,8,128]{3,2,1,0:T(8,128)} %param.8), channel_id=1, source_target_pairs={{0,16},{1,17},{4,20},{5,21},{8,24},{9,25},{12,28},{13,29},{16,32},... | collective-permute-start | bytes 1302536 | tf_op jit(solution)/shard_map/ppermute | solution.py:251
  4.3 27.3 %collective-permute-start.3 = (f32[53,2,8,128]{3,2,1,0:T(8,128)}, f32[53,2,8,128]{3,2,1,0:T(8,128)S(1)}, u32[]{:S(2)}, u32[]{:S(2)}) collective-permute-start(f32[53,2,8,128]{3,2,1,0:T(8,128)} %param.8), channel_id=1, source_target_pairs={{18,2},{19,3},{22,6},{23,7},{26,10},{27,11},{30,14},{31,15},{34,18... | collective-permute-start | bytes 1302536 | tf_op jit(solution)/shard_map/ppermute | solution.py:296
  31.6 1.1 pack.1
  32.8 1.3 %collective-permute-start.10 = (f32[2,53,128]{2,1,0:T(8,128)S(1)}, f32[2,53,128]{2,1,0:T(8,128)S(1)}, u32[]{:S(2)}, u32[]{:S(2)}) collective-permute-start(f32[2,53,128]{2,1,0:T(8,128)S(1)} %get-tuple-element.20), channel_id=1, source_target_pairs={{1023,0},{1010,1},{1011,4},{1014,5},{1015,8},{1018,9},{1019,12},{1... | collective-permute-start | bytes 162824 | tf_op jit(solution)/shard_map/ppermute | solution.py:277
  34.1 1.3 %collective-permute-start.4 = (f32[2,53,128]{2,1,0:T(8,128)S(1)}, f32[2,53,128]{2,1,0:T(8,128)S(1)}, u32[]{:S(2)}, u32[]{:S(2)}) collective-permute-start(f32[2,53,128]{2,1,0:T(8,128)S(1)} %get-tuple-element.20), channel_id=1, source_target_pairs={{0,16},{1,17},{2,18},{3,19},{4,20},{5,21},{6,22},{7,23},{8,24},{9,... | collective-permute-start | bytes 162824 | tf_op jit(solution)/shard_map/ppermute | solution.py:265
  35.4 0.9 convert_element_type.11
  36.3 0.0 copy-start.5
  36.3 6.2 %collective-permute-done.10.across_a = f32[2,53,128]{2,1,0:T(8,128)S(1)} collective-permute-done((f32[2,53,128]{2,1,0:T(8,128)S(1)}, f32[2,53,128]{2,1,0:T(8,128)S(1)}, u32[]{:S(2)}, u32[]{:S(2)}) %collective-permute-start.10) | collective-permute-done | bytes 54304 | tf_op jit(solution)/shard_map/ppermute | solution.py:277
  42.5 0.0 copy-done.2
  42.5 1.3 %collective-permute-start.2 = (f32[53,2,8,128]{3,2,1,0:T(8,128)S(1)}, f32[53,2,8,128]{3,2,1,0:T(8,128)S(1)}, u32[]{:S(2)}, u32[]{:S(2)}) collective-permute-start(f32[53,2,8,128]{3,2,1,0:T(8,128)S(1)} %copy-done.2), channel_id=1, source_target_pairs={{16,0},{17,1},{20,4},{21,5},{24,8},{25,9},{28,12},{29,13},{32,16},... | collective-permute-start | bytes 1302536 | tf_op jit(solution)/shard_map/ppermute | solution.py:257
  43.8 0.0 copy-done.6
  43.8 0.0 copy-done.5
  43.8 0.0 collective-permute-done.4.below.diag_below
  43.9 0.0 copy-start.8
  43.9 1.4 %collective-permute-start.5 = (f32[2,53,128]{2,1,0:T(8,128)S(1)}, f32[2,53,128]{2,1,0:T(8,128)S(1)}, u32[]{:S(2)}, u32[]{:S(2)}) collective-permute-start(f32[2,53,128]{2,1,0:T(8,128)S(1)} %get-tuple-element.21), channel_id=1, source_target_pairs={{16,0},{17,1},{18,2},{19,3},{20,4},{21,5},{22,6},{23,7},{24,8},{25... | collective-permute-start | bytes 162824 | tf_op jit(solution)/shard_map/ppermute | solution.py:271
  45.3 0.6 fusion.2.right
  46.0 0.7 copy-done.9
  46.6 9.5 %collective-permute-done.5.above.diag_above = f32[2,53,128]{2,1,0:T(8,128)S(1)} collective-permute-done((f32[2,53,128]{2,1,0:T(8,128)S(1)}, f32[2,53,128]{2,1,0:T(8,128)S(1)}, u32[]{:S(2)}, u32[]{:S(2)}) %collective-permute-start.5) | collective-permute-done | bytes 54304 | tf_op jit(solution)/shard_map/ppermute | solution.py:271
  56.2 1.3 %collective-permute-start.11 = (f32[2,53,128]{2,1,0:T(8,128)S(1)}, f32[2,53,128]{2,1,0:T(8,128)S(1)}, u32[]{:S(2)}, u32[]{:S(2)}) collective-permute-start(f32[2,53,128]{2,1,0:T(8,128)S(1)} %get-tuple-element.21), channel_id=1, source_target_pairs={{0,1023},{1,1010},{4,1011},{5,1014},{8,1015},{9,1018},{12,1019},{1... | collective-permute-start | bytes 162824 | tf_op jit(solution)/shard_map/ppermute | solution.py:278
  57.5 0.8 copy.14.left
  58.3 0.1 copy.13
  58.4 0.7 pad.13.rate
  59.1 1.8 %hold.1 = (bf16[328,192]{1,0:T(8,128)(2,1)}, bf16[128,328]{1,0:T(8,128)(2,1)}, f32[328,2]{1,0:T(8,128)}) custom-call(bf16[328,192]{1,0:T(8,128)(2,1)} %copy.14.left, bf16[128,328]{1,0:T(8,128)(2,1)} %fusion.2.right, f32[328,2]{1,0:T(8,128)} %pad.13.rate), custom_call_target="tpu_custom_call" | custom-call | tf_op jit(solution)/shard_map/hold/pallas_call | solution.py:302
  61.0 0.0 copy-done.1
  61.0 0.0 collective-permute-done.11.across_b
  61.0 0.0 copy-start.7
  61.0 1.9 %collective-permute-start.6 = (f32[4,53,128]{2,1,0:T(8,128)S(1)}, f32[4,53,128]{2,1,0:T(8,128)S(1)}, u32[]{:S(2)}, u32[]{:S(2)}) collective-permute-start(f32[4,53,128]{2,1,0:T(8,128)S(1)} %get-tuple-element.26), channel_id=1, source_target_pairs={{0,1},{1,0},{2,3},{3,2},{4,5},{5,4},{6,7},{7,6},{8,9},{9,8},{10,11... | collective-permute-start | bytes 325640 | tf_op jit(solution)/shard_map/ppermute | solution.py:314
  62.9 0.0 collective-permute-done.1
  62.9 28.1 %collective-permute-start.9 = (f32[4,53,128]{2,1,0:T(8,128)S(1)}, f32[4,53,128]{2,1,0:T(8,128)S(1)}, u32[]{:S(2)}, u32[]{:S(2)}) collective-permute-start(f32[4,53,128]{2,1,0:T(8,128)S(1)} %get-tuple-element.27), channel_id=1, source_target_pairs={{0,15},{1,2},{4,3},{5,6},{8,7},{9,10},{12,11},{13,14}} | collective-permute-start | bytes 325640 | tf_op jit(solution)/shard_map/ppermute | solution.py:288
  91.0 0.0 collective-permute-done
  91.0 1.3 %collective-permute-start.8 = (f32[4,53,128]{2,1,0:T(8,128)S(1)}, f32[4,53,128]{2,1,0:T(8,128)S(1)}, u32[]{:S(2)}, u32[]{:S(2)}) collective-permute-start(f32[4,53,128]{2,1,0:T(8,128)S(1)} %get-tuple-element.27), channel_id=1, source_target_pairs={{2,1},{3,4},{6,5},{7,8},{10,9},{11,12},{14,13},{15,0},{16,31},{17,... | collective-permute-start | bytes 325640 | tf_op jit(solution)/shard_map/ppermute | solution.py:288
  92.3 0.0 collective-permute-done.3
  92.4 0.7 collective-permute-start.7
  93.0 0.0 copy-done.3
  93.0 1.0 edge_0.1
  94.1 0.0 copy-done.7
  94.1 0.0 collective-permute-done.6.short
  94.1 2.2 %collective-permute-start.12 = (f32[53,128]{1,0:T(8,128)S(1)}, f32[53,128]{1,0:T(8,128)S(1)}, u32[]{:S(2)}, u32[]{:S(2)}) collective-permute-start(f32[53,128]{1,0:T(8,128)S(1)} %edge_0.1), channel_id=1, source_target_pairs={{0,1},{1,0},{4,5},{5,4},{8,9},{9,8},{12,13},{13,12}} | collective-permute-start | bytes 81416 | tf_op jit(solution)/shard_map/ppermute | solution.py:330
  96.4 0.0 collective-permute-done.9.long_c
  96.4 0.7 collective-permute-start.13
  97.0 19.9 %collective-permute-done.8.long_b = f32[4,53,128]{2,1,0:T(8,128)S(1)} collective-permute-done((f32[4,53,128]{2,1,0:T(8,128)S(1)}, f32[4,53,128]{2,1,0:T(8,128)S(1)}, u32[]{:S(2)}, u32[]{:S(2)}) %collective-permute-start.8) | collective-permute-done | bytes 108576 | tf_op jit(solution)/shard_map/ppermute | solution.py:288
  116.9 0.0 collective-permute-done.7.long_d
  116.9 0.0 collective-permute-done.2
  116.9 0.0 collective-permute-done.12.corner_0
  116.9 0.0 collective-permute-done.13.corner_1
  116.9 0.8 copy-done.4
  117.7 7.6 %step.1 = f32[848,128]{1,0:T(8,128)} custom-call(s32[2,8]{1,0:T(2,128)} %marks.1, f32[53]{0:T(128)} %spread.1, f32[848,128]{1,0:T(8,128)} %bitcast.14, f32[848,128]{1,0:T(8,128)} %bitcast.16, f32[848,128]{1,0:T(8,128)S(1)} %bitcast.10, f32[848,128]{1,0:T(8,128)} %bitcast.17, f32[848,128]{1,0:T(8,128)S(1)} %bitcast.12, ...), custom_call_target="tpu_custom_call" | custom-call | tf_op jit(solution)/shard_map/step/pallas_call | solution.py:344
  (17 shorter events, 0.1 us)
Async XLA Ops:
  0.0 42.5 %copy-start.2 = (f32[53,2,8,128]{3,2,1,0:T(8,128)S(1)}, f32[53,2,8,128]{3,2,1,0:T(8,128)}, u32[]{:S(2)}) copy-start(f32[53,2,8,128]{3,2,1,0:T(8,128)} %param.8) | copy-start | bytes 1302532
  0.0 62.9 %collective-permute-start.1 = (f32[53,2,8,128]{3,2,1,0:T(8,128)}, f32[53,2,8,128]{3,2,1,0:T(8,128)S(1)}, u32[]{:S(2)}, u32[]{:S(2)}) collective-permute-start(f32[53,2,8,128]{3,2,1,0:T(8,128)} %param.8), channel_id=1, source_target_pairs={{2,18},{3,19},{6,22},{7,23},{10,26},{11,27},{14,30},{15,31},{18,34... | collective-permute-start | bytes 1302536 | tf_op jit(solution)/shard_map/ppermute | solution.py:291
  0.8 90.2 %collective-permute-start = (f32[53,2,8,128]{3,2,1,0:T(8,128)}, f32[53,2,8,128]{3,2,1,0:T(8,128)S(1)}, u32[]{:S(2)}, u32[]{:S(2)}) collective-permute-start(f32[53,2,8,128]{3,2,1,0:T(8,128)} %param.8), channel_id=1, source_target_pairs={{0,16},{1,17},{4,20},{5,21},{8,24},{9,25},{12,28},{13,29},{16,32},... | collective-permute-start | bytes 1302536 | tf_op jit(solution)/shard_map/ppermute | solution.py:251
  4.3 88.0 %collective-permute-start.3 = (f32[53,2,8,128]{3,2,1,0:T(8,128)}, f32[53,2,8,128]{3,2,1,0:T(8,128)S(1)}, u32[]{:S(2)}, u32[]{:S(2)}) collective-permute-start(f32[53,2,8,128]{3,2,1,0:T(8,128)} %param.8), channel_id=1, source_target_pairs={{18,2},{19,3},{22,6},{23,7},{26,10},{27,11},{30,14},{31,15},{34,18... | collective-permute-start | bytes 1302536 | tf_op jit(solution)/shard_map/ppermute | solution.py:296
  32.8 9.7 %collective-permute-start.10 = (f32[2,53,128]{2,1,0:T(8,128)S(1)}, f32[2,53,128]{2,1,0:T(8,128)S(1)}, u32[]{:S(2)}, u32[]{:S(2)}) collective-permute-start(f32[2,53,128]{2,1,0:T(8,128)S(1)} %get-tuple-element.20), channel_id=1, source_target_pairs={{1023,0},{1010,1},{1011,4},{1014,5},{1015,8},{1018,9},{1019,12},{1... | collective-permute-start | bytes 162824 | tf_op jit(solution)/shard_map/ppermute | solution.py:277
  34.1 9.8 %collective-permute-start.4 = (f32[2,53,128]{2,1,0:T(8,128)S(1)}, f32[2,53,128]{2,1,0:T(8,128)S(1)}, u32[]{:S(2)}, u32[]{:S(2)}) collective-permute-start(f32[2,53,128]{2,1,0:T(8,128)S(1)} %get-tuple-element.20), channel_id=1, source_target_pairs={{0,16},{1,17},{2,18},{3,19},{4,20},{5,21},{6,22},{7,23},{8,24},{9,... | collective-permute-start | bytes 162824 | tf_op jit(solution)/shard_map/ppermute | solution.py:265
  36.3 7.5 %copy-start.5 = (s32[325,53]{0,1:T(8,128)S(1)}, s32[325,53]{0,1:T(8,128)}, u32[]{:S(2)}) copy-start(s32[325,53]{0,1:T(8,128)} %param.15) | copy-start | bytes 206704
  42.5 1.3 %copy-start.6 = (f32[2,53,128]{2,1,0:T(8,128)}, f32[2,53,128]{2,1,0:T(8,128)S(1)}, u32[]{:S(2)}) copy-start(f32[2,53,128]{2,1,0:T(8,128)S(1)} %collective-permute-done.10.across_a) | copy-start | bytes 162820
  42.5 74.4 %collective-permute-start.2 = (f32[53,2,8,128]{3,2,1,0:T(8,128)S(1)}, f32[53,2,8,128]{3,2,1,0:T(8,128)S(1)}, u32[]{:S(2)}, u32[]{:S(2)}) collective-permute-start(f32[53,2,8,128]{3,2,1,0:T(8,128)S(1)} %copy-done.2), channel_id=1, source_target_pairs={{16,0},{17,1},{20,4},{21,5},{24,8},{25,9},{28,12},{29,13},{32,16},... | collective-permute-start | bytes 1302536 | tf_op jit(solution)/shard_map/ppermute | solution.py:257
  43.9 17.1 %copy-start = (f32[2,53,128]{2,1,0:T(8,128)}, f32[2,53,128]{2,1,0:T(8,128)S(1)}, u32[]{:S(2)}) copy-start(f32[2,53,128]{2,1,0:T(8,128)S(1)} %collective-permute-done.4.below.diag_below) | copy-start | bytes 162820
  43.9 2.1 %copy-start.8 = (f32[325]{0:T(512)S(1)}, f32[325]{0:T(512)}, u32[]{:S(2)}) copy-start(f32[325]{0:T(512)} %param.12) | copy-start | bytes 3904
  43.9 12.3 %collective-permute-start.5 = (f32[2,53,128]{2,1,0:T(8,128)S(1)}, f32[2,53,128]{2,1,0:T(8,128)S(1)}, u32[]{:S(2)}, u32[]{:S(2)}) collective-permute-start(f32[2,53,128]{2,1,0:T(8,128)S(1)} %get-tuple-element.21), channel_id=1, source_target_pairs={{16,0},{17,1},{18,2},{19,3},{20,4},{21,5},{22,6},{23,7},{24,8},{25... | collective-permute-start | bytes 162824 | tf_op jit(solution)/shard_map/ppermute | solution.py:271
  46.0 0.7 copy-start.9
  56.2 4.8 %copy-start.1 = (f32[2,53,128]{2,1,0:T(8,128)}, f32[2,53,128]{2,1,0:T(8,128)S(1)}, u32[]{:S(2)}) copy-start(f32[2,53,128]{2,1,0:T(8,128)S(1)} %collective-permute-done.5.above.diag_above) | copy-start | bytes 162820
  56.2 4.8 %collective-permute-start.11 = (f32[2,53,128]{2,1,0:T(8,128)S(1)}, f32[2,53,128]{2,1,0:T(8,128)S(1)}, u32[]{:S(2)}, u32[]{:S(2)}) collective-permute-start(f32[2,53,128]{2,1,0:T(8,128)S(1)} %get-tuple-element.21), channel_id=1, source_target_pairs={{0,1023},{1,1010},{4,1011},{5,1014},{8,1015},{9,1018},{12,1019},{1... | collective-permute-start | bytes 162824 | tf_op jit(solution)/shard_map/ppermute | solution.py:278
  61.0 33.1 %copy-start.7 = (f32[2,53,128]{2,1,0:T(8,128)}, f32[2,53,128]{2,1,0:T(8,128)S(1)}, u32[]{:S(2)}) copy-start(f32[2,53,128]{2,1,0:T(8,128)S(1)} %collective-permute-done.11.across_b) | copy-start | bytes 162820
  61.0 33.1 %collective-permute-start.6 = (f32[4,53,128]{2,1,0:T(8,128)S(1)}, f32[4,53,128]{2,1,0:T(8,128)S(1)}, u32[]{:S(2)}, u32[]{:S(2)}) collective-permute-start(f32[4,53,128]{2,1,0:T(8,128)S(1)} %get-tuple-element.26), channel_id=1, source_target_pairs={{0,1},{1,0},{2,3},{3,2},{4,5},{5,4},{6,7},{7,6},{8,9},{9,8},{10,11... | collective-permute-start | bytes 325640 | tf_op jit(solution)/shard_map/ppermute | solution.py:314
  62.9 33.4 %collective-permute-start.9 = (f32[4,53,128]{2,1,0:T(8,128)S(1)}, f32[4,53,128]{2,1,0:T(8,128)S(1)}, u32[]{:S(2)}, u32[]{:S(2)}) collective-permute-start(f32[4,53,128]{2,1,0:T(8,128)S(1)} %get-tuple-element.27), channel_id=1, source_target_pairs={{0,15},{1,2},{4,3},{5,6},{8,7},{9,10},{12,11},{13,14}} | collective-permute-start | bytes 325640 | tf_op jit(solution)/shard_map/ppermute | solution.py:288
  91.0 2.0 %copy-start.3 = (f32[53,2,8,128]{3,2,1,0:T(8,128)}, f32[53,2,8,128]{3,2,1,0:T(8,128)S(1)}, u32[]{:S(2)}) copy-start(f32[53,2,8,128]{3,2,1,0:T(8,128)S(1)} %collective-permute-done) | copy-start | bytes 1302532
  91.0 25.9 %collective-permute-start.8 = (f32[4,53,128]{2,1,0:T(8,128)S(1)}, f32[4,53,128]{2,1,0:T(8,128)S(1)}, u32[]{:S(2)}, u32[]{:S(2)}) collective-permute-start(f32[4,53,128]{2,1,0:T(8,128)S(1)} %get-tuple-element.27), channel_id=1, source_target_pairs={{2,1},{3,4},{6,5},{7,8},{10,9},{11,12},{14,13},{15,0},{16,31},{17,... | collective-permute-start | bytes 325640 | tf_op jit(solution)/shard_map/ppermute | solution.py:288
  92.4 24.6 %collective-permute-start.7 = (f32[4,53,128]{2,1,0:T(8,128)S(1)}, f32[4,53,128]{2,1,0:T(8,128)S(1)}, u32[]{:S(2)}, u32[]{:S(2)}) collective-permute-start(f32[4,53,128]{2,1,0:T(8,128)S(1)} %get-tuple-element.27), channel_id=1, source_target_pairs={{1008,1023},{1009,1010},{1010,1009},{1011,1012},{1012,1011},{1013,... | collective-permute-start | bytes 325640 | tf_op jit(solution)/shard_map/ppermute | solution.py:288
  94.1 22.8 %collective-permute-start.12 = (f32[53,128]{1,0:T(8,128)S(1)}, f32[53,128]{1,0:T(8,128)S(1)}, u32[]{:S(2)}, u32[]{:S(2)}) collective-permute-start(f32[53,128]{1,0:T(8,128)S(1)} %edge_0.1), channel_id=1, source_target_pairs={{0,1},{1,0},{4,5},{5,4},{8,9},{9,8},{12,13},{13,12}} | collective-permute-start | bytes 81416 | tf_op jit(solution)/shard_map/ppermute | solution.py:330
  96.4 20.6 %collective-permute-start.13 = (f32[53,128]{1,0:T(8,128)S(1)}, f32[53,128]{1,0:T(8,128)S(1)}, u32[]{:S(2)}, u32[]{:S(2)}) collective-permute-start(f32[53,128]{1,0:T(8,128)S(1)} %edge_1.1), channel_id=1, source_target_pairs={{2,3},{3,2},{6,7},{7,6},{10,11},{11,10},{14,15},{15,14},{1008,1009... | collective-permute-start | bytes 81416 | tf_op jit(solution)/shard_map/ppermute | solution.py:338
  116.9 0.8 copy-start.4
